TPU v7x, 32 devices: a whole 2x2x4 slice. The times are simulated.
32 devices in a mesh: group: 2 (over x), tile: 16 (over z, y, core).
Axes of the slice: x: 2, y: 2, z: 4, core: 2. Of those that a mesh axis runs over, the one named last changes fastest.
Arguments:
- hadamard: int32 [128, 1152], P(None, 'tile'), may hold values from -1 to 1, as said below
- stroke: float32 [2304], P(('group', 'tile')), parts along dimension 0, may hold values from 0.3 to 1
- influence: bfloat16 [3, 2304, 8192], P(None, ('group', 'tile')), parts along dimension 1, may hold values from -0.4375 to 0.4375
- amplitude: float32 [1024, 16, 16], P(('group', 'tile')), parts along dimension 0, may hold values from 0.3 to 1
- aberration: float32 [1024, 16, 16], P(('group', 'tile')), parts along dimension 0, may hold values from -3 to 3
- valid_mask: int32 [1024], P(('group', 'tile')), parts along dimension 0, may hold values from 0 to 1, as said below
Outputs:
- imat: float32 [2304, 2, 512], P(('group', 'tile')), parts along dimension 0
There are 2 independent parts, one for each index of `group`. A program takes and returns all parts, laid end to end along the dimension named above; an argument that names none is the same for every part. Nothing has to cross between parts.
Inputs may be any that keep to these rules, and one draw needn't show every extreme that they name: `hadamard`: each column is one column of a Sylvester-Hadamard matrix whose order is the least power of two not below 1152, restricted to 128 distinct rows of it; different actuators take different columns. `valid_mask`: every pupil tile of 32 subapertures holds at least one valid subaperture.
All inputs are finite; a program needn't handle non-finite values.
Results may differ from a plain program's by a relative error of at most 0.0055.
Values may be sent and summed in bfloat16 or wider, within the bound.
No kernel may reach another device: no remote copies, remote signals or barrier semaphores. Data moves between devices by JAX's collectives and lax.ppermute only.
A program may use at most 128 MiB of HBM per device.

v0:
```python
import math

import jax
import jax.numpy as jnp
from jax import lax
from jax.sharding import PartitionSpec as P

PIX = 16


HIGHEST = lax.Precision.HIGHEST


def passed_along(value, axis, steps):
    count = lax.axis_size(axis)
    first, last = (max(0, -steps), min(count, count - steps))
    return lax.ppermute(value, axis, [(source, source + steps) for source in range(first, last)])


def shortened(x):
    return jax.tree.map(lambda a: a.astype(jnp.bfloat16) if a.dtype == jnp.float32 else a, x)


def transform_tables(samples, pixels):
    freqs = jnp.arange(pixels, dtype=jnp.float32) - pixels / 2.0
    places = jnp.arange(samples, dtype=jnp.float32)
    angle = 2.0 * jnp.pi * freqs[:, None] * places[None, :] / (2.0 * samples)
    return (jnp.cos(angle), -jnp.sin(angle))


def kron_tables(samples, pixels):
    table_real, table_imag = transform_tables(samples, pixels)
    kron_real = jnp.kron(table_real, table_real) - jnp.kron(table_imag, table_imag)
    kron_imag = jnp.kron(table_real, table_imag) + jnp.kron(table_imag, table_real)
    upper = jnp.concatenate([kron_real.T, kron_imag.T], axis=1)
    lower = jnp.concatenate([-kron_imag.T, kron_real.T], axis=1)
    transform = jnp.concatenate([upper, lower], axis=0)
    centre = jnp.arange(pixels, dtype=jnp.float32) - (pixels - 1) / 2.0
    along_u = jnp.repeat(centre, pixels)
    along_v = jnp.tile(centre, pixels)
    moments = jnp.stack([jnp.ones_like(along_u), along_u, along_v], axis=1)
    return (transform, moments)


def spot_slopes(phase_map, amplitude, aberration, valid_mask):
    patterns, sub_count, samples = (phase_map.shape[0], phase_map.shape[1], phase_map.shape[2])
    flat = samples * samples
    transform, moments = kron_tables(samples, PIX)
    half = PIX * PIX
    phase_rows = phase_map.reshape(patterns, sub_count, flat)
    amp_rows = amplitude.reshape(sub_count, flat)[None]
    abe_rows = aberration.reshape(sub_count, flat)[None]
    results = []
    for pattern_sign in (1.0, -1.0):
        angles = abe_rows + pattern_sign * phase_rows
        field = jnp.concatenate([amp_rows * jnp.cos(angles), amp_rows * jnp.sin(angles)], axis=2)
        focal = jnp.dot(field.reshape(patterns * sub_count, 2 * flat), transform, precision=HIGHEST)
        intensity = focal[:, :half] * focal[:, :half] + focal[:, half:] * focal[:, half:]
        sums = jnp.dot(intensity, moments, precision=HIGHEST)
        centroid_x = sums[:, 1] / sums[:, 0]
        centroid_y = sums[:, 2] / sums[:, 0]
        results.append(
            jnp.stack([centroid_x, centroid_y], axis=1)
            .reshape(patterns, sub_count, 2)
            .transpose(0, 2, 1)
        )
    weights = valid_mask.astype(jnp.float32)[None, None, :]
    return ((results[0] - results[1]) * 0.5 * weights).astype(jnp.bfloat16)


def shape_term(commands, slab):
    term = jnp.dot(commands, slab, preferred_element_type=jnp.float32).astype(jnp.bfloat16)
    return lax.optimization_barrier(term)


def per_device(hadamard, stroke, influence, amplitude, aberration, valid_mask):
    patterns = hadamard.shape[0]
    sub_count = amplitude.shape[0]
    samples = amplitude.shape[1]
    commands = (stroke[None, :] * hadamard.astype(jnp.float32)).astype(jnp.bfloat16)
    local_term = shape_term(commands, influence[1])
    lower_cmds, lower_slab = passed_along((commands, influence[2]), "tile", 1)
    upper_cmds, upper_slab = passed_along((commands, influence[0]), "tile", -1)
    from_lower = shape_term(lower_cmds, lower_slab)
    from_upper = shape_term(upper_cmds, upper_slab)
    phase_map = (
        local_term.astype(jnp.float32)
        + from_lower.astype(jnp.float32)
        + from_upper.astype(jnp.float32)
    )
    block_rows = math.gcd(patterns, 64)
    blocks = phase_map.reshape(patterns // block_rows, block_rows, sub_count, samples, samples)

    def one_block(pattern_block):
        return spot_slopes(pattern_block, amplitude, aberration, valid_mask)

    slopes = lax.map(one_block, blocks).reshape(patterns, 2, sub_count)
    signs_half = hadamard.astype(jnp.bfloat16)
    summed = jnp.einsum(
        "pa,pcs->acs",
        signs_half,
        lax.all_gather(shortened(slopes), "tile", axis=2, tiled=True),
        preferred_element_type=jnp.float32,
    )
    return summed / (patterns * stroke)[:, None, None]


def solution(mesh):
    placed = (
        P(None, "tile"),
        P(("group", "tile")),
        P(None, ("group", "tile"), None),
        P(("group", "tile"), None, None),
        P(("group", "tile"), None, None),
        P(("group", "tile")),
    )
    return jax.shard_map(
        per_device,
        mesh=mesh,
        in_specs=placed,
        out_specs=P(("group", "tile"), None, None),
        check_vma=False,
    )
```

profile of v0, /device:TPU:0, one launch (start us, length us, event | category | flops | bytes accessed | tf_op | source)
XLA Modules:
  0.0 236.9 jit_solution(5249718799039673560)
XLA Ops:
  0.0 2.8 %slice_bitcast_fusion.1 = (bf16[72,8192]{1,0:T(8,128)(2,1)}, bf16[72,8192]{1,0:T(8,128)(2,1)S(1)}) fusion(bf16[3,72,8192]{2,1,0:T(8,128)(2,1)} %param.10), kind=kLoop, calls=%fused_computation.58 | loop fusion | bytes 4718592 | tf_op jit(solution)/shard_map/squeeze | solution.py:82
  2.8 3.6 %collective-permute-start.1 = (bf16[72,8192]{1,0:T(8,128)(2,1)}, bf16[72,8192]{1,0:T(8,128)(2,1)}, u32[]{:S(2)}, u32[]{:S(2)}) collective-permute-start(bf16[72,8192]{1,0:T(8,128)(2,1)} %get-tuple-element.136), channel_id=1, source_target_pairs={{0,1},{1,2},{2,3},{3,4},{4,5},{5,6},{6,7},{7,8},{8,9},{9,10},{10,1... | collective-permute-start | bytes 3538952 | tf_op jit(solution)/shard_map/ppermute | solution.py:17
  7.8 4.1 %collective-permute-start = (bf16[128,72]{0,1:T(8,128)(2,1)S(1)}, bf16[128,72]{0,1:T(8,128)(2,1)S(1)}, u32[]{:S(2)}, u32[]{:S(2)}) collective-permute-start(bf16[128,72]{0,1:T(8,128)(2,1)S(1)} %multiply_convert_fusion), channel_id=1, source_target_pairs={{0,1},{1,2},{2,3},{3,4},{4,5},{5,6},{6,7},{7,8},{8,9},{9,10},{10,1... | collective-permute-start | bytes 55304 | tf_op jit(solution)/shard_map/ppermute | solution.py:17
  13.2 2.0 convolution_convert_fusion.2
  15.3 2.0 convolution_convert_fusion.1
  17.3 2.0 convolution_convert_fusion
  19.3 2.8 %convert_add_fusion = f32[128,8192]{1,0:T(8,128)} fusion(bf16[128,8192]{1,0:T(8,128)(2,1)S(1)} %convolution_convert_fusion, bf16[128,8192]{1,0:T(8,128)(2,1)S(1)} %convolution_convert_fusion.1, bf16[128,8192]{1,0:T(8,128)(2,1)S(1)} %convolution_convert_fusion.2), kind=kLoop, calls=%fused_computation.55 | loop fusion | flops 5242880 | bytes 10485760 | tf_op jit(solution)/shard_map/add | solution.py:87
  22.1 5.6 %copy.28 = f32[128,8192]{0,1:T(8,128)} copy(f32[128,8192]{1,0:T(8,128)} %convert_add_fusion) | data formatting | bytes 8388608 | tf_op jit(solution)/shard_map/add | solution.py:87
  27.7 9.2 %reshape.211 = f32[2,64,32,16,16]{1,0,4,3,2:T(2,128)} reshape(f32[128,8192]{0,1:T(8,128)} %copy.28) | data formatting | bytes 8388608 | tf_op jit(solution)/shard_map/reshape | solution.py:92
  36.9 159.1 %while.12 = (s32[]{:T(128)}, bf16[2,64,2,32]{1,0,3,2:T(2,128)(2,1)S(1)}, f32[32,16,16]{0,2,1:T(8,128)S(1)}, f32[32,16,16]{0,2,1:T(8,128)S(1)}, f32[2,64,32,16,16...) while((s32[]{:T(128)}, ...), condition=%wide.region_1.2_spmd, body=%wide.region_0.1_spmd.sunk | while | flops 12933627904 | bytes 64969588 | solution.py:97
  36.9 9.7 %constant_dynamic-slice_fusion.2 = f32[1,64,32,16,16]{1,0,4,3,2:T(1,128)} fusion(f32[2,64,32,16,16]{1,0,4,3,2:T(2,128)} %get-tuple-element.223, s32[]{:T(128)} %get-tuple-element.209), kind=kLoop, calls=%fused_computation.46.clone.1 | loop fusion | bytes 4194308 | tf_op jit(solution)/shard_map/while/body/jit(dynamic_index_in_dim)/dynamic_slice | solution.py:97
  46.6 12.3 %copy.40 = f32[1,64,32,16,16]{2,1,4,3,0:T(8,128)} copy(f32[1,64,32,16,16]{1,0,4,3,2:T(1,128)} %constant_dynamic-slice_fusion.2) | data formatting | bytes 4194304 | tf_op jit(solution)/shard_map/while/body/jit(dynamic_index_in_dim)/dynamic_slice | solution.py:97
  58.9 7.5 %reshape.239 = f32[2048,256]{0,1:T(8,128)} reshape(f32[1,64,32,16,16]{2,1,4,3,0:T(8,128)} %copy.40) | data formatting | bytes 4194304 | tf_op jit(solution)/shard_map/while/body/eval_jaxpr/reshape | solution.py:50
  66.4 1.9 copy.41
  68.5 16.6 %bitcast_multiply_fusion.5 = (f32[2048,256]{1,0:T(8,128)}, f32[2048,256]{1,0:T(8,128)}, f32[2048,256]{1,0:T(8,128)}, f32[2048,256]{1,0:T(8,128)}) fusion(f32[2048,256]{1,0:T(8,128)S(1)} %copy.41, f32[32,256]{1,0:T(8,128)S(1)} %copy.42, f32[32,256]{1,0:T(8,128)S(1)} %copy.43), kind=kLoop, calls=%fused_computation.3.clone.1 | loop fusion | flops 3670016 | bytes 10551296 | tf_op jit(solution)/shard_map/while/body/eval_jaxpr/mul | solution.py:56
  85.3 2.0 multiply_add_fusion.2
  87.2 2.4 %add.133 = f32[256,256]{1,0:T(8,128)S(1)} reshape(f32[16,16,16,16]{3,2,1,0:T(8,128)} %get-tuple-element.192) | data formatting | bytes 524288 | tf_op jit(solution)/shard_map/while/body/eval_jaxpr/add | solution.py:34
  90.7 9.8 %fusion.57 = f32[2048,512]{1,0:T(8,128)} fusion(f32[2048,256]{1,0:T(8,128)} %get-tuple-element.193, f32[2048,256]{1,0:T(8,128)} %get-tuple-element.194, f32[256,256]{0,1:T(8,128)S(1)} %bitcast.82, f32[256,256]{0,1:T(8,128)S(1)} %bitcast_negate_fusion.2, f32[256,256]{0,1:T(8,128)S(1)} %bitcast.80), kind=kOutput, calls=%fused_computation.8.clone.1 | convolution fusion | flops 6444285952 | bytes 9175040 | tf_op jit(solution)/shard_map/while/body/eval_jaxpr/dot_general | solution.py:57
  100.7 4.4 %fusion.58 = f32[2048,3]{0,1:T(4,128)S(1)} fusion(f32[2048,512]{1,0:T(8,128)} %fusion.57, f32[256,1]{0,1:T(1,128)S(1)} %tile.19, f32[256,1]{0,1:T(1,128)S(1)} %reshape.240, f32[3]{0:T(128)S(1)} %pad.6.clone.2), kind=kOutput, calls=%fused_computation.16.clone.1 | convolution fusion | flops 20448768 | bytes 4220940 | tf_op jit(solution)/shard_map/while/body/eval_jaxpr/dot_general | solution.py:59
  105.1 8.5 %fusion.55 = f32[2048,512]{1,0:T(8,128)S(1)} fusion(f32[2048,256]{1,0:T(8,128)} %get-tuple-element.187, f32[2048,256]{1,0:T(8,128)S(1)} %copy-done, f32[256,256]{0,1:T(8,128)S(1)} %bitcast.83, f32[256,256]{0,1:T(8,128)S(1)} %bitcast_negate_fusion.2, f32[256,256]{0,1:T(8,128)S(1)} %bitcast.81), kind=kOutput, calls=%fused_computation.4.clone.1 | convolution fusion | flops 6444285952 | bytes 9175040 | tf_op jit(solution)/shard_map/while/body/eval_jaxpr/dot_general | solution.py:57
  113.6 2.0 fusion.56
  116.5 9.7 %constant_dynamic-slice_fusion.2 = f32[1,64,32,16,16]{1,0,4,3,2:T(1,128)} fusion(f32[2,64,32,16,16]{1,0,4,3,2:T(2,128)} %get-tuple-element.223, s32[]{:T(128)} %get-tuple-element.209), kind=kLoop, calls=%fused_computation.46.clone.1 | loop fusion | bytes 4194308 | tf_op jit(solution)/shard_map/while/body/jit(dynamic_index_in_dim)/dynamic_slice | solution.py:97
  126.2 12.3 %copy.40 = f32[1,64,32,16,16]{2,1,4,3,0:T(8,128)} copy(f32[1,64,32,16,16]{1,0,4,3,2:T(1,128)} %constant_dynamic-slice_fusion.2) | data formatting | bytes 4194304 | tf_op jit(solution)/shard_map/while/body/jit(dynamic_index_in_dim)/dynamic_slice | solution.py:97
  138.5 7.5 %reshape.239 = f32[2048,256]{0,1:T(8,128)} reshape(f32[1,64,32,16,16]{2,1,4,3,0:T(8,128)} %copy.40) | data formatting | bytes 4194304 | tf_op jit(solution)/shard_map/while/body/eval_jaxpr/reshape | solution.py:50
  148.1 16.6 %bitcast_multiply_fusion.5 = (f32[2048,256]{1,0:T(8,128)}, f32[2048,256]{1,0:T(8,128)}, f32[2048,256]{1,0:T(8,128)}, f32[2048,256]{1,0:T(8,128)}) fusion(f32[2048,256]{1,0:T(8,128)S(1)} %copy.41, f32[32,256]{1,0:T(8,128)S(1)} %copy.42, f32[32,256]{1,0:T(8,128)S(1)} %copy.43), kind=kLoop, calls=%fused_computation.3.clone.1 | loop fusion | flops 3670016 | bytes 10551296 | tf_op jit(solution)/shard_map/while/body/eval_jaxpr/mul | solution.py:56
  164.8 2.0 multiply_add_fusion.2
  166.8 2.4 %add.133 = f32[256,256]{1,0:T(8,128)S(1)} reshape(f32[16,16,16,16]{3,2,1,0:T(8,128)} %get-tuple-element.192) | data formatting | bytes 524288 | tf_op jit(solution)/shard_map/while/body/eval_jaxpr/add | solution.py:34
  170.2 9.8 %fusion.57 = f32[2048,512]{1,0:T(8,128)} fusion(f32[2048,256]{1,0:T(8,128)} %get-tuple-element.193, f32[2048,256]{1,0:T(8,128)} %get-tuple-element.194, f32[256,256]{0,1:T(8,128)S(1)} %bitcast.82, f32[256,256]{0,1:T(8,128)S(1)} %bitcast_negate_fusion.2, f32[256,256]{0,1:T(8,128)S(1)} %bitcast.80), kind=kOutput, calls=%fused_computation.8.clone.1 | convolution fusion | flops 6444285952 | bytes 9175040 | tf_op jit(solution)/shard_map/while/body/eval_jaxpr/dot_general | solution.py:57
  180.3 4.4 %fusion.58 = f32[2048,3]{0,1:T(4,128)S(1)} fusion(f32[2048,512]{1,0:T(8,128)} %fusion.57, f32[256,1]{0,1:T(1,128)S(1)} %tile.19, f32[256,1]{0,1:T(1,128)S(1)} %reshape.240, f32[3]{0:T(128)S(1)} %pad.6.clone.2), kind=kOutput, calls=%fused_computation.16.clone.1 | convolution fusion | flops 20448768 | bytes 4220940 | tf_op jit(solution)/shard_map/while/body/eval_jaxpr/dot_general | solution.py:59
  184.7 8.5 %fusion.55 = f32[2048,512]{1,0:T(8,128)S(1)} fusion(f32[2048,256]{1,0:T(8,128)} %get-tuple-element.187, f32[2048,256]{1,0:T(8,128)S(1)} %copy-done, f32[256,256]{0,1:T(8,128)S(1)} %bitcast.83, f32[256,256]{0,1:T(8,128)S(1)} %bitcast_negate_fusion.2, f32[256,256]{0,1:T(8,128)S(1)} %bitcast.81), kind=kOutput, calls=%fused_computation.4.clone.1 | convolution fusion | flops 6444285952 | bytes 9175040 | tf_op jit(solution)/shard_map/while/body/eval_jaxpr/dot_general | solution.py:57
  193.2 2.0 fusion.56
  196.1 39.6 %all_gather.3 = bf16[128,2,512]{0,2,1:T(8,128)(2,1)S(1)} all-gather(bf16[128,2,32]{0,2,1:T(8,128)(2,1)S(1)} %reshape.212), channel_id=1, replica_groups=mesh['group'=2,'tile'=16] {'tile'}, dimensions={2}, use_global_device_ids=true | all-gather | bytes 278528 | tf_op jit(solution)/shard_map/all_gather | solution.py:102
  (70 shorter events, 10.4 us)
Async XLA Ops:
  0.0 7.7 %copy-start.3 = (s32[128,72]{0,1:T(8,128)S(1)}, s32[128,72]{0,1:T(8,128)}, u32[]{:S(2)}) copy-start(s32[128,72]{0,1:T(8,128)} %param.8) | copy-start | bytes 110596
  0.0 7.7 %copy-start.4 = (f32[72]{0:T(128)S(1)}, f32[72]{0:T(128)}, u32[]{:S(2)}) copy-start(f32[72]{0:T(128)} %param.9) | copy-start | bytes 868
  2.8 12.4 %copy-start.5 = (s32[32]{0:T(128)S(1)}, s32[32]{0:T(128)}, u32[]{:S(2)}) copy-start(s32[32]{0:T(128)} %param.13) | copy-start | bytes 388
  2.8 12.4 %collective-permute-start.1 = (bf16[72,8192]{1,0:T(8,128)(2,1)}, bf16[72,8192]{1,0:T(8,128)(2,1)}, u32[]{:S(2)}, u32[]{:S(2)}) collective-permute-start(bf16[72,8192]{1,0:T(8,128)(2,1)} %get-tuple-element.136), channel_id=1, source_target_pairs={{0,1},{1,2},{2,3},{3,4},{4,5},{5,6},{6,7},{7,8},{8,9},{9,10},{10,1... | collective-permute-start | bytes 3538952 | tf_op jit(solution)/shard_map/ppermute | solution.py:17
  6.4 10.9 %collective-permute-start.3 = (bf16[72,8192]{1,0:T(8,128)(2,1)S(1)}, bf16[72,8192]{1,0:T(8,128)(2,1)}, u32[]{:S(2)}, u32[]{:S(2)}) collective-permute-start(bf16[72,8192]{1,0:T(8,128)(2,1)S(1)} %get-tuple-element.137), channel_id=1, source_target_pairs={{1,0},{2,1},{3,2},{4,3},{5,4},{6,5},{7,6},{8,7},{9,8},{10,9},{11,1... | collective-permute-start | bytes 3538952 | tf_op jit(solution)/shard_map/ppermute | solution.py:17
  7.8 7.5 %collective-permute-start = (bf16[128,72]{0,1:T(8,128)(2,1)S(1)}, bf16[128,72]{0,1:T(8,128)(2,1)S(1)}, u32[]{:S(2)}, u32[]{:S(2)}) collective-permute-start(bf16[128,72]{0,1:T(8,128)(2,1)S(1)} %multiply_convert_fusion), channel_id=1, source_target_pairs={{0,1},{1,2},{2,3},{3,4},{4,5},{5,6},{6,7},{7,8},{8,9},{9,10},{10,1... | collective-permute-start | bytes 55304 | tf_op jit(solution)/shard_map/ppermute | solution.py:17
  11.9 5.4 %collective-permute-start.2 = (bf16[128,72]{0,1:T(8,128)(2,1)S(1)}, bf16[128,72]{0,1:T(8,128)(2,1)S(1)}, u32[]{:S(2)}, u32[]{:S(2)}) collective-permute-start(bf16[128,72]{0,1:T(8,128)(2,1)S(1)} %multiply_convert_fusion), channel_id=1, source_target_pairs={{1,0},{2,1},{3,2},{4,3},{5,4},{6,5},{7,6},{8,7},{9,8},{10,9},{11,1... | collective-permute-start | bytes 55304 | tf_op jit(solution)/shard_map/ppermute | solution.py:17
  27.7 9.2 %copy-start.1 = (f32[32,16,16]{0,2,1:T(8,128)S(1)}, f32[32,16,16]{0,2,1:T(8,128)}, u32[]{:S(2)}) copy-start(f32[32,16,16]{0,2,1:T(8,128)} %param.11) | copy-start | bytes 98308
  27.7 9.2 %copy-start.2 = (f32[32,16,16]{0,2,1:T(8,128)S(1)}, f32[32,16,16]{0,2,1:T(8,128)}, u32[]{:S(2)}) copy-start(f32[32,16,16]{0,2,1:T(8,128)} %param.12) | copy-start | bytes 98308
  100.5 4.7 %copy-start = (f32[2048,256]{1,0:T(8,128)S(1)}, f32[2048,256]{1,0:T(8,128)}, u32[]{:S(2)}) copy-start(f32[2048,256]{1,0:T(8,128)} %get-tuple-element.188) | copy-start | bytes 6291460 | tf_op jit(solution)/shard_map/while
  180.0 4.7 %copy-start = (f32[2048,256]{1,0:T(8,128)S(1)}, f32[2048,256]{1,0:T(8,128)}, u32[]{:S(2)}) copy-start(f32[2048,256]{1,0:T(8,128)} %get-tuple-element.188) | copy-start | bytes 6291460 | tf_op jit(solution)/shard_map/while
where the time goes:
time: 238 us; the launch traced here: 237 us
  local copies, waits for them, and re-layouts  90.3 us (38%)
  matrix products  55.7 us (23%)
  other arithmetic  40.7 us (17%)
  blocking collectives  39.6 us (17%)
  starting transfers between devices  10.3 us (4%)
    dynamic_slice x4, local copies, waits for them, and re-layouts, per_device(): slopes = lax.map(one_block, blocks).reshape(patterns, 2, sub_count)  44.1 us
    all_gather x1, blocking collectives, per_device(): lax.all_gather(shortened(slopes), 'tile', axis=2, tiled=True)  39.6 us
    dot_general x4, matrix products, spot_slopes(): jnp.dot(field.reshape(patterns * sub_count, 2 * flat), transform, precisi...  36.6 us
    mul x2, other arithmetic, spot_slopes(): amp_rows * jnp.cos(angles)  33.3 us
    reshape x4, local copies, waits for them, and re-layouts, spot_slopes(): phase_rows = phase_map.reshape(patterns, sub_count, flat)  18.8 us
    dot_general x4, matrix products, spot_slopes(): sums = jnp.dot(intensity, moments, precision=HIGHEST)  12.9 us
    ppermute x4, starting transfers between devices, passed_along(): lax.ppermute(value, axis, [(source, source + steps) for source in range(f...  10.3 us
    reshape x1, local copies, waits for them, and re-layouts, per_device(): phase_map.reshape(patterns // block_rows, block_rows, sub_count, samples,...  9.2 us
  transfers between devices with their start and end apart: 4, of which 0 were waited for; matrix products, arithmetic and copies ran while one was open for 2% of the time, Pallas kernels for 0%

commit v1 on v0

v1 whole, which is shorter than its diff:
```python
import math

import jax
import jax.numpy as jnp
import numpy as np
from jax import lax
from jax.experimental import pallas as pl
from jax.experimental.pallas import tpu as pltpu
from jax.sharding import PartitionSpec as P

PIX = 16


def half_turn_tables():
    nodes = 0.125 * (1.0 - np.cos(np.pi * (np.arange(200) + 0.5) / 200))
    r = np.sqrt(nodes)
    sin_fit = np.polynomial.chebyshev.Chebyshev.fit(
        nodes, math.sqrt(2) * np.sin(np.pi * r) / r, 4, domain=[0, 0.25]
    ).convert(kind=np.polynomial.Polynomial)
    cos_fit = np.polynomial.chebyshev.Chebyshev.fit(
        nodes, math.sqrt(2) * np.cos(np.pi * r), 5, domain=[0, 0.25]
    ).convert(kind=np.polynomial.Polynomial)
    return [float(c) for c in sin_fit.coef], [float(c) for c in cos_fit.coef]


SIN_FIT, COS_FIT = half_turn_tables()


def horner(coefs, z):
    value = z * coefs[-1] + coefs[-2]
    for c in coefs[-3::-1]:
        value = value * z + c
    return value


def cos_sin(phase):
    turns = phase * (1.0 / (2.0 * math.pi))
    r = turns - jnp.round(turns)
    z = r * r
    half_sin = horner(SIN_FIT, z) * r
    half_cos = horner(COS_FIT, z)
    return 1.0 - half_sin * half_sin, half_sin * half_cos


def dft_tables(samples, pixels):
    freqs = np.arange(pixels) - pixels / 2.0
    table = np.exp(-2j * np.pi * freqs[:, None] * np.arange(samples)[None, :] / (2.0 * samples))
    full = np.kron(table, table)
    return full.real.astype(np.float32), full.imag.astype(np.float32)


def subaperture_transforms(amplitude, aberration):
    subs, samples = amplitude.shape[0], amplitude.shape[1]
    real, imag = dft_tables(samples, PIX)
    amp = amplitude.reshape(subs, 1, samples * samples)
    abe = aberration.reshape(subs, 1, samples * samples)
    field_re, field_im = amp * jnp.cos(abe), amp * jnp.sin(abe)
    first = jnp.asarray(np.concatenate([real, imag]))[None]
    second = jnp.asarray(np.concatenate([-imag, real]))[None]
    return (first * field_re + second * field_im).astype(jnp.bfloat16)


def spots_kernel(per_step, mask_ref, cmd_a, cmd_b, cmd_c, slab_a, slab_b, slab_c, trans_ref, out_ref, cmds, sums):
    step = pl.program_id(0)
    half = PIX * PIX
    flat = trans_ref.shape[2]

    @pl.when(step == 0)
    def _():
        for k, ref in enumerate((cmd_a, cmd_b, cmd_c)):
            cmds[k] = ref[...].astype(jnp.float32).T.astype(jnp.bfloat16)

    patterns = out_ref.shape[2]
    for s in range(per_step):
        cols = slice(s * flat, (s + 1) * flat)
        phase = None
        for k, ref in enumerate((slab_a, slab_b, slab_c)):
            rows = ref[0, :, cols] if len(ref.shape) == 3 else ref[:, cols]
            term = jnp.dot(cmds[k], rows, preferred_element_type=jnp.float32)
            term = term.astype(jnp.bfloat16).astype(jnp.float32)
            phase = term if phase is None else phase + term
        waves = jnp.concatenate([w.astype(jnp.bfloat16) for w in cos_sin(phase)], axis=0)
        focal = lax.dot_general(
            trans_ref[s], waves, (((1,), (1,)), ((), ())), preferred_element_type=jnp.float32
        )
        ur, vr = focal[:half, :patterns], focal[:half, patterns:]
        ui, vi = focal[half:, :patterns], focal[half:, patterns:]
        even = (ur * ur + ui * ui) + (vr * vr + vi * vi)
        odd = ui * vr - ur * vi
        for k, value in enumerate((even, odd)):
            grid = value.reshape(PIX, PIX // 8, 8, patterns)
            along_u = along_v = None
            for u in range(PIX):
                line = grid[u]
                along_v = line if along_v is None else along_v + line
                total = line[0] + line[1]
                moved = total * (u - (PIX - 1) / 2.0)
                along_u = moved if along_u is None else along_u + moved
            sums[k, 0, s] = along_v[0] + along_v[1]
            sums[k, 1, s] = along_u
            below = lax.broadcasted_iota(jnp.int32, (8, patterns), 0).astype(jnp.float32)
            lead = -(PIX - 1) / 2.0
            sums[k, 2, s] = along_v[0] * (below + lead) + along_v[1] * (below + (lead + 8))
    total = jnp.sum(sums[...], axis=3)
    even, odd = total[0], 2.0 * total[1]
    scale = 1.0 / ((even[0] + odd[0]) * (even[0] - odd[0]))
    for c in range(2):
        slope = (odd[1 + c] * even[0] - even[1 + c] * odd[0]) * scale
        for s in range(per_step):
            valid = mask_ref[step * per_step + s].astype(jnp.float32)
            out_ref[c, pl.ds(s, 1), :] = (slope[s : s + 1] * valid).astype(out_ref.dtype)


def spot_slopes(mask, cmds, slabs, transform, first, count, per_step):
    half, flat = transform.shape[1], transform.shape[2]
    acts, patterns = cmds[0].shape
    width = per_step * flat
    skip = first // per_step

    def slab_spec(slab, offset):
        if slab.ndim == 3:
            return pl.BlockSpec((1, acts, width), lambda i: (1, 0, i + offset))
        return pl.BlockSpec((acts, width), lambda i: (0, i + offset))

    return pl.pallas_call(
        lambda *refs: spots_kernel(per_step, *refs),
        grid=(count // per_step,),
        in_specs=[pl.BlockSpec(memory_space=pltpu.SMEM)]
        + [pl.BlockSpec((acts, patterns), lambda i: (0, 0))] * 3
        + [slab_spec(slabs[0], skip), slab_spec(slabs[1], skip), slab_spec(slabs[2], 0)]
        + [pl.BlockSpec((per_step, half, flat), lambda i: (i + skip, 0, 0))],
        out_specs=pl.BlockSpec((2, per_step, patterns), lambda i: (0, i, 0)),
        out_shape=jax.ShapeDtypeStruct((2, count, patterns), jnp.bfloat16),
        scratch_shapes=[
            pltpu.VMEM((3, patterns, acts), jnp.bfloat16),
            pltpu.VMEM((2, 3, per_step, 8, patterns), jnp.float32),
        ],
        name="spots",
    )(mask, *cmds, *slabs, transform)


def pairings(count):
    near = [(i, i ^ 1) for i in range(count) if (i ^ 1) < count]
    far = [(i, i + 1 if i % 2 else i - 1) for i in range(count)]
    return near, [(a, b) for a, b in far if 0 <= b < count]


def per_device(hadamard, stroke, influence, amplitude, aberration, valid_mask):
    count = lax.axis_size("tile")
    parity = lax.axis_index("tile") % 2
    patterns, acts = hadamard.shape
    subs = amplitude.shape[0]
    points = influence.shape[2]
    signs = hadamard.T.astype(jnp.float32)
    commands = (stroke[:, None] * signs).astype(jnp.bfloat16)
    near, far = pairings(count)
    far_slab = lax.dynamic_slice_in_dim(influence, 2 * parity, 1, 0)[0]
    near_slab = lax.dynamic_slice_in_dim(influence, 2 - 2 * parity, 1, 0)[0]
    far_sent = lax.ppermute(jnp.concatenate([far_slab, commands], axis=1), "tile", far)
    near_sent = lax.ppermute(jnp.concatenate([near_slab, commands], axis=1), "tile", near)
    transform = subaperture_transforms(amplitude, aberration)
    cmds = (commands, near_sent[:, points:], far_sent[:, points:])
    slopes = spot_slopes(valid_mask, cmds, (influence, near_sent, far_sent), transform, 0, subs, 8)
    gathered = lax.all_gather(slopes, "tile", axis=1, tiled=True)
    summed = jnp.einsum(
        "ap,csp->acs", signs.astype(jnp.bfloat16), gathered, preferred_element_type=jnp.float32
    )
    return summed / (patterns * stroke)[:, None, None]


def solution(mesh):
    placed = (
        P(None, "tile"),
        P(("group", "tile")),
        P(None, ("group", "tile"), None),
        P(("group", "tile"), None, None),
        P(("group", "tile"), None, None),
        P(("group", "tile")),
    )
    return jax.shard_map(
        per_device,
        mesh=mesh,
        in_specs=placed,
        out_specs=P(("group", "tile"), None, None),
        check_vma=False,
    )
```

time: 238 us -> 72.8 us (0.31)
  local copies, waits for them, and re-layouts: 90.3 us -> 6.47 us
  matrix products: 55.7 us -> 0.29 us
  other arithmetic: 40.7 us -> 9.63 us
  Pallas kernels: 0 us -> 12.2 us
  starting transfers between devices: 10.3 us -> 1.22 us
  blocking collectives: 39.6 us -> 42.6 us
    dot_general x12 -> x1, matrix products: 55.7 us -> 0.29 us  [per_device(): jnp.einsum('ap,csp->acs', signs.astype(jnp.bfloat16), gathered, preferred...]
    dynamic_slice x4 -> x0, local copies, waits for them, and re-layouts: 44.1 us -> none  [per_device(): slopes = lax.map(one_block, blocks).reshape(patterns, 2, sub_count)]
    mul x6 -> x1, other arithmetic: 33.3 us -> 1.17 us  [subaperture_transforms(): field_re, field_im = (amp * jnp.cos(abe), amp * jnp.sin(abe))]
    reshape x8 -> x0, local copies, waits for them, and re-layouts: 28.3 us -> none  [the longest x4 18.8 us: spot_slopes(): phase_rows = phase_map.reshape(patterns, sub_count, flat)]
    pallas_call x0 -> x1, Pallas kernels: none -> 12.2 us  [spot_slopes(): pl.pallas_call(lambda *refs: spots_kernel(per_step, *refs), grid=(count /...]
    add x5 -> x0, local copies, waits for them, and re-layouts: 10.6 us -> none  [the longest x1 5.57 us: per_device(): local_term.astype(jnp.float32) + from_lower.astype(jnp.float32)]
    ppermute x4 -> x2, starting transfers between devices: 10.3 us -> 1.22 us  [the longest x1 0.73 us: per_device(): lax.ppermute(jnp.concatenate([far_slab, commands], axis=1), 'tile', far)]
    add x3 -> x0, other arithmetic: 6.76 us -> none  [the longest x2 3.97 us: kron_tables(): jnp.kron(table_real, table_imag) + jnp.kron(table_imag, table_real)]
  transfers between devices with their start and end apart: 4 -> 2, of which waited for: 0 -> 0; matrix products, arithmetic and copies ran while one was open for 2% -> 13% of each run, Pallas kernels for 0% -> 0%
where the time goes in v1:
time: 72.8 us; the launch traced here: 72.5 us
  blocking collectives  42.6 us (59%)
  Pallas kernels  12.2 us (17%)
  other arithmetic  9.63 us (13%)
  local copies, waits for them, and re-layouts  6.47 us (9%)
  starting transfers between devices  1.22 us (2%)
    all_gather x1, blocking collectives, per_device(): gathered = lax.all_gather(slopes, 'tile', axis=1, tiled=True)  42.6 us
    pallas_call x1, Pallas kernels, spot_slopes(): pl.pallas_call(lambda *refs: spots_kernel(per_step, *refs), grid=(count /...  12.2 us
    convert_element_type x1, other arithmetic, subaperture_transforms(): return (first * field_re + second * field_im).astype(jnp.bfloat16)  5.94 us
    mul x2, local copies, waits for them, and re-layouts, subaperture_transforms(): field_re, field_im = (amp * jnp.cos(abe), amp * jnp.sin(abe))  1.94 us
    squeeze x1, local copies, waits for them, and re-layouts, per_device(): far_slab = lax.dynamic_slice_in_dim(influence, 2 * parity, 1, 0)[0]  1.83 us
    concatenate x1, other arithmetic, per_device(): jnp.concatenate([far_slab, commands], axis=1)  1.67 us
  transfers between devices with their start and end apart: 2, of which 0 were waited for; matrix products, arithmetic and copies ran while one was open for 13% of the time, Pallas kernels for 0%

profile of v1, /device:TPU:0, one launch (start us, length us, event | category | flops | bytes accessed | tf_op | source)
XLA Modules:
  0.0 72.5 jit_solution(11585050784421724902)
XLA Ops:
  0.0 0.8 %fusion.3.refs_1_ = bf16[72,128]{1,0:T(8,128)(2,1)S(1)} fusion(s32[128,72]{0,1:T(8,128)} %param.8, f32[72]{0:T(128)} %param.9), kind=kLoop, calls=%fused_computation.12 | loop fusion | flops 27648 | bytes 55584 | tf_op jit(solution)/shard_map/convert_element_type | solution.py:155
  0.8 0.0 copy-start.4
  0.9 1.8 %dynamic-slice_bitcast_fusion = (bf16[72,8192]{1,0:T(8,128)(2,1)S(1)}, bf16[72,8192]{1,0:T(8,128)(2,1)S(1)}) fusion(bf16[3,72,8192]{2,1,0:T(8,128)(2,1)} %refs_4_.1, s32[]{:T(128)S(6)} %select_n.15, s32[]{:T(128)S(6)} %select_n.14), kind=kLoop, calls=%fused_computation.3 | loop fusion | bytes 4718600 | tf_op jit(solution)/shard_map/squeeze | solution.py:157
  2.7 0.0 copy-start.5
  2.7 0.0 copy-start.6
  2.7 0.0 copy-start.8
  2.7 0.0 copy-start.2
  2.7 0.0 copy-start.3
  2.8 1.7 %pad_maximum_fusion = (bf16[72,8320]{1,0:T(8,128)(2,1)}, bf16[72,8320]{1,0:T(8,128)(2,1)}) fusion(bf16[72,128]{1,0:T(8,128)(2,1)S(1)} %fusion.3.refs_1_, bf16[72,8192]{1,0:T(8,128)(2,1)S(1)} %get-tuple-element.5, bf16[72,8192]{1,0:T(8,128)(2,1)S(1)} %get-tuple-element.6), kind=kLoop, calls=%fused_computation.1 | loop fusion | flops 4193280 | bytes 4773888 | tf_op jit(solution)/shard_map/concatenate | solution.py:159
  4.4 0.0 copy-done.4
  4.4 0.5 collective-permute-start
  4.9 0.7 %collective-permute-start.1 = (bf16[72,8320]{1,0:T(8,128)(2,1)}, bf16[72,8320]{1,0:T(8,128)(2,1)S(1)}, u32[]{:S(2)}, u32[]{:S(2)}) collective-permute-start(bf16[72,8320]{1,0:T(8,128)(2,1)} %get-tuple-element.9), channel_id=1, source_target_pairs={{1,2},{2,1},{3,4},{4,3},{5,6},{6,5},{7,8},{8,7},{9,10},{10,9},{11,... | collective-permute-start | bytes 3594248 | tf_op jit(solution)/shard_map/ppermute | solution.py:159
  5.7 0.0 copy-done.5
  5.7 0.0 copy-done.6
  5.7 1.2 %cosine_multiply_fusion = (f32[32,16,16]{0,2,1:T(8,128)}, f32[32,16,16]{0,2,1:T(8,128)}) fusion(f32[32,16,16]{0,2,1:T(8,128)S(1)} %copy-done.5, f32[32,16,16]{0,2,1:T(8,128)S(1)} %copy-done.6), kind=kLoop, calls=%fused_computation.8 | loop fusion | flops 16384 | bytes 131072 | tf_op jit(solution)/shard_map/mul | solution.py:57
  6.8 1.0 %copy.10 = f32[32,256]{1,0:T(8,128)S(1)} copy(f32[32,256]{0,1:T(8,128)} %bitcast.15) | data formatting | bytes 65536 | tf_op jit(solution)/shard_map/mul | solution.py:57
  7.8 1.0 %copy.9 = f32[32,256]{1,0:T(8,128)S(1)} copy(f32[32,256]{0,1:T(8,128)} %bitcast.14) | data formatting | bytes 65536 | tf_op jit(solution)/shard_map/mul | solution.py:57
  8.8 0.0 copy-done.8
  8.8 0.0 copy-done.2
  8.8 0.0 copy-done.3
  8.8 5.9 %add_convert_fusion.refs_7_ = bf16[32,512,256]{2,1,0:T(8,128)(2,1)} fusion(f32[32,256]{1,0:T(8,128)S(1)} %copy.10, f32[512,256]{1,0:T(8,128)S(1)} %copy-done.3, f32[32,256]{1,0:T(8,128)S(1)} %copy.9, f32[512,256]{1,0:T(8,128)S(1)} %copy-done.2), kind=kLoop, calls=%fused_computation | loop fusion | flops 16777216 | bytes 9502720 | tf_op jit(solution)/shard_map/convert_element_type | solution.py:60
  14.8 0.0 collective-permute-done.refs_5_
  14.8 0.6 slice.8.refs_2_
  15.4 0.0 collective-permute-done.1.refs_6_
  15.4 0.6 slice.9.refs_3_
  16.1 0.0 copy-done
  16.1 0.4 copy-done.1
  16.5 12.2 %spots.1 = bf16[2,32,128]{2,1,0:T(8,128)(2,1)} custom-call(s32[32]{0:T(128)} %refs_0_.1, bf16[72,128]{1,0:T(8,128)(2,1)} %copy-done.4, bf16[72,128]{1,0:T(8,128)(2,1)} %slice.8.refs_2_, bf16[72,128]{1,0:T(8,128)(2,1)} %slice.9.refs_3_, bf16[3,72,8192]{2,1,0:T(8,128)(2,1)} %refs_4_.1, bf16[72,8320]{1,0:T(8,128)(2,1)} %copy-done, bf16[72,8320]{1,0:T(8,128)(2,1)} %copy-done.1, ...), custom_call_target="tpu_custom_call" | custom-call | tf_op jit(solution)/shard_map/spots/pallas_call | solution.py:125
  28.6 42.6 %all_gather.3 = bf16[2,512,128]{2,1,0:T(8,128)(2,1)S(1)} all-gather(bf16[2,32,128]{2,1,0:T(8,128)(2,1)} %spots.1), channel_id=1, replica_groups=mesh['group'=2,'tile'=16] {'tile'}, dimensions={1}, use_global_device_ids=true | all-gather | bytes 278528 | tf_op jit(solution)/shard_map/all_gather | solution.py:164
  71.3 0.0 copy-done.7
  71.3 0.3 fusion
  71.6 0.9 %copy.11 = f32[72,2,512]{2,1,0:T(2,128)} copy(f32[72,2,512]{2,0,1:T(8,128)S(1)} %fusion) | data formatting | bytes 589824 | tf_op jit(solution)/shard_map/div | solution.py:168
  (4 shorter events, 0.0 us)
Async XLA Ops:
  0.8 3.6 %copy-start.4 = (bf16[72,128]{1,0:T(8,128)(2,1)}, bf16[72,128]{1,0:T(8,128)(2,1)S(1)}, u32[]{:S(2)}) copy-start(bf16[72,128]{1,0:T(8,128)(2,1)S(1)} %fusion.3.refs_1_) | copy-start | bytes 55300
  2.7 3.0 %copy-start.5 = (f32[32,16,16]{0,2,1:T(8,128)S(1)}, f32[32,16,16]{0,2,1:T(8,128)}, u32[]{:S(2)}) copy-start(f32[32,16,16]{0,2,1:T(8,128)} %param.11) | copy-start | bytes 98308
  2.7 3.0 %copy-start.6 = (f32[32,16,16]{0,2,1:T(8,128)S(1)}, f32[32,16,16]{0,2,1:T(8,128)}, u32[]{:S(2)}) copy-start(f32[32,16,16]{0,2,1:T(8,128)} %param.12) | copy-start | bytes 98308
  2.7 6.1 %copy-start.8 = (f32[72]{0:T(128)S(1)}, f32[72]{0:T(128)}, u32[]{:S(2)}) copy-start(f32[72]{0:T(128)} %param.9) | copy-start | bytes 868
  2.7 6.1 %copy-start.2 = (f32[512,256]{1,0:T(8,128)S(1)}, f32[512,256]{1,0:T(8,128)}, u32[]{:S(2)}) copy-start(f32[512,256]{1,0:T(8,128)} %constant.28.clone) | copy-start | bytes 1572868
  2.7 6.1 %copy-start.3 = (f32[512,256]{1,0:T(8,128)S(1)}, f32[512,256]{1,0:T(8,128)}, u32[]{:S(2)}) copy-start(f32[512,256]{1,0:T(8,128)} %constant.29.clone) | copy-start | bytes 1572868
  4.4 10.3 %collective-permute-start = (bf16[72,8320]{1,0:T(8,128)(2,1)}, bf16[72,8320]{1,0:T(8,128)(2,1)S(1)}, u32[]{:S(2)}, u32[]{:S(2)}) collective-permute-start(bf16[72,8320]{1,0:T(8,128)(2,1)} %get-tuple-element.10), channel_id=1, source_target_pairs={{0,1},{1,0},{2,3},{3,2},{4,5},{5,4},{6,7},{7,6},{8,9},{9,8},{10,11... | collective-permute-start | bytes 3594248 | tf_op jit(solution)/shard_map/ppermute | solution.py:160
  4.9 10.5 %collective-permute-start.1 = (bf16[72,8320]{1,0:T(8,128)(2,1)}, bf16[72,8320]{1,0:T(8,128)(2,1)S(1)}, u32[]{:S(2)}, u32[]{:S(2)}) collective-permute-start(bf16[72,8320]{1,0:T(8,128)(2,1)} %get-tuple-element.9), channel_id=1, source_target_pairs={{1,2},{2,1},{3,4},{4,3},{5,6},{6,5},{7,8},{8,7},{9,10},{10,9},{11,... | collective-permute-start | bytes 3594248 | tf_op jit(solution)/shard_map/ppermute | solution.py:159
  14.8 1.3 %copy-start = (bf16[72,8320]{1,0:T(8,128)(2,1)}, bf16[72,8320]{1,0:T(8,128)(2,1)S(1)}, u32[]{:S(2)}) copy-start(bf16[72,8320]{1,0:T(8,128)(2,1)S(1)} %collective-permute-done.refs_5_) | copy-start | bytes 3594244
  15.4 1.1 %copy-start.1 = (bf16[72,8320]{1,0:T(8,128)(2,1)}, bf16[72,8320]{1,0:T(8,128)(2,1)S(1)}, u32[]{:S(2)}) copy-start(bf16[72,8320]{1,0:T(8,128)(2,1)S(1)} %collective-permute-done.1.refs_6_) | copy-start | bytes 3594244
  16.5 54.8 %copy-start.7 = (s32[128,72]{0,1:T(8,128)S(1)}, s32[128,72]{0,1:T(8,128)}, u32[]{:S(2)}) copy-start(s32[128,72]{0,1:T(8,128)} %param.8) | copy-start | bytes 110596

commit v2 on v1

v2 whole, which is shorter than its diff:
```python
import math

import jax
import jax.numpy as jnp
import numpy as np
from jax import lax
from jax.experimental import pallas as pl
from jax.experimental.pallas import tpu as pltpu
from jax.sharding import PartitionSpec as P


PIX = 16
LANES = 8
GROUP = 4


def power_fit(values, nodes, degree):
    fit = np.polynomial.chebyshev.Chebyshev.fit(nodes, values, degree, domain=[0, 0.25])
    return [float(c) for c in fit.convert(kind=np.polynomial.Polynomial).coef]


def half_turn_fits():
    nodes = 0.125 * (1.0 - np.cos(np.pi * (np.arange(200) + 0.5) / 200))
    r = np.sqrt(nodes)
    root = math.sqrt(2.0)
    return (
        power_fit(root * np.sin(np.pi * r) / r, nodes, 3),
        power_fit(root * np.cos(np.pi * r), nodes, 4),
    )


SIN_FIT, COS_FIT = half_turn_fits()


def horner(coefs, z):
    value = z * coefs[-1] + coefs[-2]
    for c in coefs[-3::-1]:
        value = value * z + c
    return value


def cos_sin(phase):
    turns = phase * (1.0 / (2.0 * math.pi))
    r = turns - jnp.round(turns)
    z = r * r
    half_sin = horner(SIN_FIT, z) * r
    half_cos = horner(COS_FIT, z)
    return 1.0 - half_sin * half_sin, half_sin * half_cos


def dft_table(samples, pixels):
    freqs = np.arange(pixels) - pixels / 2.0
    table = np.exp(-2j * np.pi * freqs[:, None] * np.arange(samples)[None, :] / (2.0 * samples))
    full = np.kron(table, table)
    return np.concatenate([full.real, full.imag]).astype(np.float32)


def bf16_term(commands, slab):
    term = jnp.dot(commands, slab, preferred_element_type=jnp.float32)
    return term.astype(jnp.bfloat16).astype(jnp.float32)


def turned(ref_value):
    return ref_value.astype(jnp.float32).T.astype(jnp.bfloat16)


def prepare_kernel(
    cmds_ref, near_ref, amp_ref, abe_ref, table_ref, influence, trans_ref, phase_ref, field, own_slab, cmds, arrival
):
    subs, flat = trans_ref.shape[0], trans_ref.shape[2]
    half = trans_ref.shape[1] // 2
    fetch = pltpu.make_async_copy(influence.at[1], own_slab, arrival)
    fetch.start()
    cosine, sine = cos_sin(abe_ref[...])
    field[0] = (amp_ref[...] * cosine).T
    field[1] = (amp_ref[...] * sine).T
    cmds[0] = turned(cmds_ref[...])
    cmds[1] = turned(near_ref[:, subs * flat :])

    def fold(s, carry):
        real, imag = field[0, pl.ds(s, 1), :], field[1, pl.ds(s, 1), :]
        real = jnp.broadcast_to(real, (2 * LANES, flat))
        imag = jnp.broadcast_to(imag, (2 * LANES, flat))
        for row in range(0, half, 2 * LANES):
            upper, lower = table_ref[row : row + 2 * LANES], table_ref[half + row : half + row + 2 * LANES]
            trans_ref[s, row : row + 2 * LANES] = (upper * real - lower * imag).astype(jnp.bfloat16)
            trans_ref[s, half + row : half + row + 2 * LANES] = (lower * real + upper * imag).astype(jnp.bfloat16)
        return carry

    lax.fori_loop(0, subs, fold, 0)
    fetch.wait()

    def add_terms(g, carry):
        for k in range(GROUP):
            s = g * GROUP + k
            cols = pl.ds(pl.multiple_of(s * flat, flat), flat)
            phase_ref[s] = bf16_term(cmds[0], own_slab[:, cols]) + bf16_term(cmds[1], near_ref[:, cols])
        return carry

    lax.fori_loop(0, subs // GROUP, add_terms, 0)


def prepare(commands, near_sent, influence, amplitude, aberration):
    subs, samples = amplitude.shape[0], amplitude.shape[1]
    flat = samples * samples
    acts, patterns = commands.shape
    table = jnp.asarray(dft_table(samples, PIX))
    half = table.shape[0]
    whole = pl.BlockSpec(memory_space=pltpu.VMEM)
    return pl.pallas_call(
        prepare_kernel,
        in_specs=[whole] * 5 + [pl.BlockSpec(memory_space=pl.ANY)],
        out_specs=[whole] * 2,
        out_shape=[
            jax.ShapeDtypeStruct((subs, half, flat), jnp.bfloat16),
            jax.ShapeDtypeStruct((subs, patterns, flat), jnp.float32),
        ],
        scratch_shapes=[
            pltpu.VMEM((2, subs, flat), jnp.float32),
            pltpu.VMEM((acts, subs * flat), jnp.bfloat16),
            pltpu.VMEM((2, patterns, acts), jnp.bfloat16),
            pltpu.SemaphoreType.DMA,
        ],
        compiler_params=pltpu.CompilerParams(vmem_limit_bytes=8 << 20),
        cost_estimate=pl.CostEstimate(flops=10**9, bytes_accessed=8 << 20, transcendentals=0),
        name="prepare",
    )(
        commands,
        near_sent,
        amplitude.reshape(subs, flat).T,
        aberration.reshape(subs, flat).T,
        table,
        influence,
    )


def running_moments(values):
    middle = (PIX - 1) / 2.0
    low, high, steps = values[0][0], values[0][1], None
    for u in range(1, PIX):
        both = low + high
        steps = both if steps is None else steps + both
        low = low + values[u][0]
        high = high + values[u][1]
    total = low + high
    row = lax.broadcasted_iota(jnp.int32, total.shape, 0).astype(jnp.float32)
    return total, total * middle - steps, low * (row - middle) + high * (row + (LANES - middle))


def spots_kernel(first, lead, done, mask_ref, cmds_ref, slab_ref, trans_ref, phase_ref, *refs):
    earlier, refs = refs[:done], refs[done:]
    out_ref, refs = refs[0], refs[1:]
    sums = refs[-1]
    flat = trans_ref.shape[2]
    patterns = out_ref.shape[2]
    count = sums.shape[2]
    if lead:
        cmds = refs[0]
        cmds[...] = turned(cmds_ref[:, count * flat :])
    else:
        cmds = cmds_ref

    def group(g, carry):
        for k in range(GROUP):
            s = g * GROUP + k
            cols = pl.ds(pl.multiple_of(s * flat, flat), flat)
            phase = phase_ref[first + s] + bf16_term(cmds[...], slab_ref[:, cols])
            waves = jnp.concatenate([w.astype(jnp.bfloat16) for w in cos_sin(phase)], axis=0)
            focal = lax.dot_general(
                trans_ref[first + s],
                waves,
                (((1,), (1,)), ((), ())),
                preferred_element_type=jnp.float32,
            )
            lines = focal.reshape(2, PIX, PIX // LANES, LANES, 2 * patterns)
            even, odd = [], []
            for u in range(PIX):
                even.append([])
                odd.append([])
                for v in range(PIX // LANES):
                    ur, vr = lines[0, u, v, :, :patterns], lines[0, u, v, :, patterns:]
                    ui, vi = lines[1, u, v, :, :patterns], lines[1, u, v, :, patterns:]
                    even[u].append((ur * ur + ui * ui) + (vr * vr + vi * vi))
                    odd[u].append(ui * vr - ur * vi)
            for kind, values in enumerate((even, odd)):
                for m, value in enumerate(running_moments(values)):
                    sums[kind, m, s] = value
        return carry

    lax.fori_loop(0, count // GROUP, group, 0)
    total = jnp.sum(sums[...], axis=3)
    even, odd = total[0], 2.0 * total[1]
    scale = 1.0 / ((even[0] + odd[0]) * (even[0] - odd[0]))
    row = lax.broadcasted_iota(jnp.int32, (count, patterns), 0)
    valid = jnp.zeros((count, patterns), jnp.float32)
    for s in range(count):
        valid = jnp.where(row == s, mask_ref[first + s].astype(jnp.float32), valid)
    scale = scale * valid
    for c in range(2):
        slope = ((odd[1 + c] * even[0] - even[1 + c] * odd[0]) * scale).astype(out_ref.dtype)
        pieces = [ref[c] for ref in earlier] + [slope]
        out_ref[c] = jnp.concatenate(pieces, axis=0) if earlier else slope


def spot_slopes(mask, cmds, slab, transform, phase, first, count, earlier):
    acts = slab.shape[0]
    patterns = phase.shape[1]
    lead = cmds is None
    rows = count + sum(part.shape[1] for part in earlier)
    whole = pl.BlockSpec(memory_space=pltpu.VMEM)
    out_shape = [jax.ShapeDtypeStruct((2, rows, patterns), jnp.bfloat16)]
    if lead:
        out_shape.append(jax.ShapeDtypeStruct((patterns, acts), jnp.bfloat16))
    return pl.pallas_call(
        lambda *refs: spots_kernel(first, lead, len(earlier), *refs),
        in_specs=[pl.BlockSpec(memory_space=pltpu.SMEM)] + [whole] * (4 + len(earlier)),
        out_specs=[whole] * len(out_shape),
        out_shape=out_shape,
        scratch_shapes=[pltpu.VMEM((2, 3, count, LANES, patterns), jnp.float32)],
        compiler_params=pltpu.CompilerParams(vmem_limit_bytes=8 << 20),
        cost_estimate=pl.CostEstimate(flops=10**8 * count, bytes_accessed=10**6, transcendentals=0),
        name="spots",
    )(mask, slab if lead else cmds, slab, transform, phase, *earlier)


def decode_kernel(parity_ref, signs_ref, stroke_ref, same_ref, other_ref, out_ref):
    pairs, rows, patterns = same_ref.shape
    acts = signs_ref.shape[0]
    subs = rows // 2
    signs = signs_ref[...].astype(jnp.float32).astype(jnp.bfloat16)
    scale = jnp.broadcast_to(1.0 / (stroke_ref[...] * patterns), (LANES, acts)).T[:, :1]

    def write(even_ref, odd_ref):
        for c in range(2):
            part = slice(c * subs, (c + 1) * subs)
            slopes = jnp.stack([even_ref[:, part, :], odd_ref[:, part, :]], axis=1)
            summed = lax.dot_general(
                signs,
                slopes.reshape(2 * pairs * subs, patterns),
                (((1,), (1,)), ((), ())),
                preferred_element_type=jnp.float32,
            )
            out_ref[:, c, :] = summed * scale

    pl.when(parity_ref[0] == 0)(lambda: write(same_ref, other_ref))
    pl.when(parity_ref[0] == 1)(lambda: write(other_ref, same_ref))


def decode(parity, signs, stroke, same, other):
    pairs, rows, _ = same.shape
    acts = signs.shape[0]
    return pl.pallas_call(
        decode_kernel,
        in_specs=[pl.BlockSpec(memory_space=pltpu.SMEM)] + [pl.BlockSpec(memory_space=pltpu.VMEM)] * 4,
        out_specs=pl.BlockSpec(memory_space=pltpu.VMEM),
        out_shape=jax.ShapeDtypeStruct((acts, 2, pairs * rows), jnp.float32),
        compiler_params=pltpu.CompilerParams(vmem_limit_bytes=8 << 20),
        name="decode",
    )(parity.reshape(1), signs, stroke.reshape(1, acts), same, other)


def pairings(count):
    near = [(i, i ^ 1) for i in range(count) if (i ^ 1) < count]
    far = [(i, i + 1 if i % 2 else i - 1) for i in range(count)]
    return near, [(a, b) for a, b in far if 0 <= b < count]


def chunk_sizes(subs):
    unit = subs // 8
    return [3 * unit, 2 * unit, 2 * unit, unit]


def interaction(hadamard, stroke, influence, amplitude, aberration, valid_mask):
    count = lax.axis_size("tile")
    parity = lax.axis_index("tile") % 2
    acts = stroke.shape[0]
    subs = amplitude.shape[0]
    flat = influence.shape[2] // subs
    near, far = pairings(count)
    sizes = chunk_sizes(subs)
    firsts = [sum(sizes[:k]) for k in range(len(sizes))]
    commands = (stroke[:, None] * hadamard.T.astype(jnp.float32)).astype(jnp.bfloat16)

    def slab_of(offset, first, size):
        return lax.dynamic_slice(influence, (offset, 0, first * flat), (1, acts, size * flat))[0]

    far_slabs = []
    for k, (first, size) in enumerate(zip(firsts, sizes)):
        sent = slab_of(2 * parity, first, size)
        if k == 0:
            sent = jnp.concatenate([sent, commands], axis=1)
        far_slabs.append(lax.ppermute(sent, "tile", far))
    sent = jnp.concatenate([slab_of(2 - 2 * parity, 0, subs), commands], axis=1)
    near_sent = lax.ppermute(sent, "tile", near)
    transform, phase = prepare(commands, near_sent, influence, amplitude, aberration)
    parts, far_cmds = [], None
    for k, (first, size) in enumerate(zip(firsts, sizes)):
        earlier = parts if k == len(sizes) - 1 else []
        found = spot_slopes(valid_mask, far_cmds, far_slabs[k], transform, phase, first, size, earlier)
        parts.append(found[0])
        if k == 0:
            far_cmds = found[1]
    slopes = parts[-1].reshape(2 * subs, -1)
    groups = [list(range(side, count, 2)) for side in range(2)]
    copies = jnp.broadcast_to(slopes, (count // 2, *slopes.shape))
    same = lax.all_to_all(copies, "tile", 0, 0, axis_index_groups=groups)
    other = lax.ppermute(same, "tile", near)
    return decode(parity, hadamard.T, stroke, same, other)


def solution(mesh):
    placed = (
        P(None, "tile"),
        P(("group", "tile")),
        P(None, ("group", "tile"), None),
        P(("group", "tile"), None, None),
        P(("group", "tile"), None, None),
        P(("group", "tile")),
    )
    return jax.shard_map(
        interaction,
        mesh=mesh,
        in_specs=placed,
        out_specs=P(("group", "tile"), None, None),
        check_vma=False,
    )
```

time: 72.8 us -> 55.1 us (0.76)
  blocking collectives: 42.6 us -> 27 us
  other arithmetic: 9.63 us -> 2.81 us
  Pallas kernels: 12.2 us -> 18 us
  local copies, waits for them, and re-layouts: 6.47 us -> 2.26 us
  starting transfers between devices: 1.22 us -> 3.21 us
  waiting for transfers between devices: 0.01 us -> 1.36 us
    all_gather x1 -> x0, blocking collectives: 42.6 us -> none  [per_device(): gathered = lax.all_gather(slopes, 'tile', axis=1, tiled=True)]
    all_to_all x0 -> x1, blocking collectives: none -> 27 us  [interaction(): same = lax.all_to_all(copies, 'tile', 0, 0, axis_index_groups=groups)]
    convert_element_type x2 -> x1, other arithmetic: 6.78 us -> 0.85 us  [interaction(): (stroke[:, None] * hadamard.T.astype(jnp.float32)).astype(jnp.bfloat16)]
    pallas_call x1 -> x6, Pallas kernels: 12.2 us -> 18 us  [the longest x4 11 us: spot_slopes(): pl.pallas_call(lambda *refs: spots_kernel(first, lead, len(earlier), *ref...]
    ppermute x2 -> x6, starting transfers between devices: 1.22 us -> 3.21 us  [the longest x4 2.72 us: interaction(): far_slabs.append(lax.ppermute(sent, 'tile', far))]
    mul x2 -> x0, local copies, waits for them, and re-layouts: 1.94 us -> none  [subaperture_transforms(): field_re, field_im = (amp * jnp.cos(abe), amp * jnp.sin(abe))]
    ppermute x2 -> x6, waiting for transfers between devices: 0.01 us -> 1.36 us  [the longest x1 1.35 us: interaction(): other = lax.ppermute(same, 'tile', near)]
    slice x2 -> x0, local copies, waits for them, and re-layouts: 1.28 us -> none  [per_device(): cmds = (commands, near_sent[:, points:], far_sent[:, points:])]
  transfers between devices with their start and end apart: 2 -> 6, of which waited for: 0 -> 1; matrix products, arithmetic and copies ran while one was open for 13% -> 2% of each run, Pallas kernels for 0% -> 28%
where the time goes in v2:
time: 55.1 us; the launch traced here: 54.9 us
  blocking collectives  27 us (49%)
  Pallas kernels  18 us (33%)
  starting transfers between devices  3.21 us (6%)
  other arithmetic  2.81 us (5%)
  local copies, waits for them, and re-layouts  2.26 us (4%)
  waiting for transfers between devices  1.36 us (2%)
    all_to_all x1, blocking collectives, interaction(): same = lax.all_to_all(copies, 'tile', 0, 0, axis_index_groups=groups)  27 us
    pallas_call x4, Pallas kernels, spot_slopes(): pl.pallas_call(lambda *refs: spots_kernel(first, lead, len(earlier), *ref...  11 us
    pallas_call x1, Pallas kernels, prepare(): pl.pallas_call(prepare_kernel, in_specs=[whole] * 5 + [pl.BlockSpec(memor...  6.08 us
    ppermute x4, starting transfers between devices, interaction(): far_slabs.append(lax.ppermute(sent, 'tile', far))  2.72 us
    squeeze x4, local copies, waits for them, and re-layouts, slab_of(): lax.dynamic_slice(influence, (offset, 0, first * flat), (1, acts, size *...  1.6 us
    ppermute x1, waiting for transfers between devices, interaction(): other = lax.ppermute(same, 'tile', near)  1.35 us
    concatenate x1, other arithmetic, interaction(): sent = jnp.concatenate([slab_of(2 - 2 * parity, 0, subs), commands], axis=1)  1.15 us
  transfers between devices with their start and end apart: 6, of which 1 were waited for; matrix products, arithmetic and copies ran while one was open for 2% of the time, Pallas kernels for 28%

profile of v2, /device:TPU:0, one launch (start us, length us, event | category | flops | bytes accessed | tf_op | source)
XLA Modules:
  0.0 54.9 jit_solution(17826241409989698628)
XLA Ops:
  0.0 1.5 %dynamic-slice_bitcast_fusion = bf16[72,8192]{1,0:T(8,128)(2,1)S(1)} fusion(bf16[3,72,8192]{2,1,0:T(8,128)(2,1)} %influence.1, s32[]{:T(128)S(6)} %select_n.18), kind=kLoop, calls=%fused_computation.1 | loop fusion | bytes 2359300 | tf_op jit(solution)/shard_map/squeeze | solution.py:285
  1.5 0.0 copy-done.8
  1.5 0.8 %multiply_convert_fusion.cmds_ref = bf16[72,128]{1,0:T(8,128)(2,1)S(1)} fusion(f32[72]{0:T(128)S(1)} %copy-done.8, s32[128,72]{0,1:T(8,128)} %param.7), kind=kLoop, calls=%fused_computation.7 | loop fusion | flops 27648 | bytes 55584 | tf_op jit(solution)/shard_map/convert_element_type | solution.py:282
  2.4 0.6 %copy-done.2 = bf16[72,128]{1,0:T(8,128)(2,1)} copy-done((bf16[72,128]{1,0:T(8,128)(2,1)}, bf16[72,128]{1,0:T(8,128)(2,1)S(1)}, u32[]{:S(2)}) %copy-start.2) | copy-done | bytes 18456
  3.0 1.1 %pad_maximum_fusion = bf16[72,8320]{1,0:T(8,128)(2,1)} fusion(bf16[72,128]{1,0:T(8,128)(2,1)S(1)} %multiply_convert_fusion.cmds_ref, bf16[72,8192]{1,0:T(8,128)(2,1)S(1)} %dynamic-slice_bitcast_fusion), kind=kLoop, calls=%fused_computation | loop fusion | flops 2396160 | bytes 2396160 | tf_op jit(solution)/shard_map/concatenate | solution.py:293
  4.1 0.5 collective-permute-start.1
  4.6 0.0 copy-done
  4.6 0.0 copy-start.6
  4.7 0.8 %pad_maximum_fusion.1 = bf16[72,3200]{1,0:T(8,128)(2,1)S(1)} fusion(bf16[72,128]{1,0:T(8,128)(2,1)} %copy-done.2, bf16[72,3072]{1,0:T(8,128)(2,1)S(1)} %dynamic-slice_bitcast_fusion.1), kind=kLoop, calls=%fused_computation.2 | loop fusion | flops 921600 | bytes 921600 | tf_op jit(solution)/shard_map/concatenate | solution.py:291
  5.5 0.7 %collective-permute-start = (bf16[72,3200]{1,0:T(8,128)(2,1)S(1)}, bf16[72,3200]{1,0:T(8,128)(2,1)S(1)}, u32[]{:S(2)}, u32[]{:S(2)}) collective-permute-start(bf16[72,3200]{1,0:T(8,128)(2,1)S(1)} %pad_maximum_fusion.1), channel_id=1, source_target_pairs={{1,2},{2,1},{3,4},{4,3},{5,6},{6,5},{7,8},{8,7},{9,10},{10,9},{11,... | collective-permute-start | bytes 1382408 | tf_op jit(solution)/shard_map/ppermute | solution.py:292
  6.3 0.7 %collective-permute-start.4 = (bf16[72,2048]{1,0:T(8,128)(2,1)S(1)}, bf16[72,2048]{1,0:T(8,128)(2,1)S(1)}, u32[]{:S(2)}, u32[]{:S(2)}) collective-permute-start(bf16[72,2048]{1,0:T(8,128)(2,1)S(1)} %get-tuple-element.13), channel_id=1, source_target_pairs={{1,2},{2,1},{3,4},{4,3},{5,6},{6,5},{7,8},{8,7},{9,10},{10,9},{11,... | collective-permute-start | bytes 884744 | tf_op jit(solution)/shard_map/ppermute | solution.py:292
  6.9 0.7 %collective-permute-start.3 = (bf16[72,2048]{1,0:T(8,128)(2,1)S(1)}, bf16[72,2048]{1,0:T(8,128)(2,1)S(1)}, u32[]{:S(2)}, u32[]{:S(2)}) collective-permute-start(bf16[72,2048]{1,0:T(8,128)(2,1)S(1)} %get-tuple-element.14), channel_id=1, source_target_pairs={{1,2},{2,1},{3,4},{4,3},{5,6},{6,5},{7,8},{8,7},{9,10},{10,9},{11,... | collective-permute-start | bytes 884744 | tf_op jit(solution)/shard_map/ppermute | solution.py:292
  7.7 0.7 %collective-permute-start.2 = (bf16[72,1024]{1,0:T(8,128)(2,1)S(1)}, bf16[72,1024]{1,0:T(8,128)(2,1)S(1)}, u32[]{:S(2)}, u32[]{:S(2)}) collective-permute-start(bf16[72,1024]{1,0:T(8,128)(2,1)S(1)} %dynamic-slice_bitcast_fusion.4), channel_id=1, source_target_pairs={{1,2},{2,1},{3,4},{4,3},{5,6},{6,5},{7,8},{8,7},{9,10},{10,9},{11,... | collective-permute-start | bytes 442376 | tf_op jit(solution)/shard_map/ppermute | solution.py:292
  8.3 0.0 collective-permute-done.1.near_ref
  8.3 0.0 copy-done.1
  8.4 0.0 copy-done.3
  8.4 0.0 copy-start.7
  8.4 6.1 %prepare.1 = (bf16[32,512,256]{2,1,0:T(8,128)(2,1)S(1)}, f32[32,128,256]{2,1,0:T(8,128)S(1)}) custom-call(bf16[72,128]{1,0:T(8,128)(2,1)S(1)} %copy-done.3, bf16[72,8320]{1,0:T(8,128)(2,1)} %collective-permute-done.1.near_ref, f32[256,32]{1,0:T(8,128)S(1)} %bitcast.22, f32[256,32]{1,0:T(8,128)S(1)} %bitcast.23, f32[512,256]{1,0:T(8,128)S(1)} %copy-done.1, ...), custom_call_target="tpu_custom_call" | custom-call | flops 1000000000 | bytes 8388608 | tf_op jit(solution)/shard_map/prepare/pallas_call | solution.py:110
  14.5 0.0 collective-permute-done.refs_1_.refs_2_
  14.5 0.0 copy-done.7
  14.5 3.9 %spots.4 = (bf16[2,12,128]{2,1,0:T(8,128)(2,1)S(1)}, bf16[128,72]{1,0:T(8,128)(2,1)S(1)}) custom-call(s32[32]{0:T(128)S(1)} %copy-done.7, bf16[72,3200]{1,0:T(8,128)(2,1)S(1)} %collective-permute-done.refs_1_.refs_2_, bf16[72,3200]{1,0:T(8,128)(2,1)S(1)} %collective-permute-done.refs_1_.refs_2_, bf16[32,512,256]{2,1,0:T(8,128)(2,1)S(1)} %get-tuple-element.9.refs_3_, ...), custom_call_target="tpu_custom_call" | custom-call | flops 1200000000 | bytes 1000000 | tf_op jit(solution)/shard_map/spots/pallas_call | solution.py:214
  18.4 0.0 collective-permute-done.4.refs_2_
  18.4 2.7 %spots.6.refs_7_ = bf16[2,8,128]{2,1,0:T(8,128)(2,1)S(1)} custom-call(s32[32]{0:T(128)S(1)} %copy-done.7, bf16[128,72]{1,0:T(8,128)(2,1)S(1)} %get-tuple-element.11.refs_1_, bf16[72,2048]{1,0:T(8,128)(2,1)S(1)} %collective-permute-done.4.refs_2_, bf16[32,512,256]{2,1,0:T(8,128)(2,1)S(1)} %get-tuple-element.9.refs_3_, ...), custom_call_target="tpu_custom_call" | custom-call | flops 800000000 | bytes 1000000 | tf_op jit(solution)/shard_map/spots/pallas_call | solution.py:214
  21.1 0.0 collective-permute-done.3.refs_2_
  21.1 2.7 %spots.5.refs_6_ = bf16[2,8,128]{2,1,0:T(8,128)(2,1)S(1)} custom-call(s32[32]{0:T(128)S(1)} %copy-done.7, bf16[128,72]{1,0:T(8,128)(2,1)S(1)} %get-tuple-element.11.refs_1_, bf16[72,2048]{1,0:T(8,128)(2,1)S(1)} %collective-permute-done.3.refs_2_, bf16[32,512,256]{2,1,0:T(8,128)(2,1)S(1)} %get-tuple-element.9.refs_3_, ...), custom_call_target="tpu_custom_call" | custom-call | flops 800000000 | bytes 1000000 | tf_op jit(solution)/shard_map/spots/pallas_call | solution.py:214
  23.8 0.0 collective-permute-done.2.refs_2_
  23.8 0.0 copy-start.4
  23.8 1.7 %spots.7 = bf16[2,32,128]{2,1,0:T(8,128)(2,1)S(1)} custom-call(s32[32]{0:T(128)S(1)} %copy-done.7, bf16[128,72]{1,0:T(8,128)(2,1)S(1)} %get-tuple-element.11.refs_1_, bf16[72,1024]{1,0:T(8,128)(2,1)S(1)} %collective-permute-done.2.refs_2_, bf16[32,512,256]{2,1,0:T(8,128)(2,1)S(1)} %get-tuple-element.9.refs_3_, ...), custom_call_target="tpu_custom_call" | custom-call | flops 400000000 | bytes 1000000 | tf_op jit(solution)/shard_map/spots/pallas_call | solution.py:214
  25.6 27.0 %all_to_all.5.same_ref = bf16[8,64,128]{2,1,0:T(8,128)(2,1)S(1)} all-to-all(bf16[8,64,128]{2,1,0:T(8,128)(2,1)S(1)} %broadcast_in_dim.4), channel_id=1, replica_groups={{0,2,4,6,8,10,12,14},{1,3,5,7,9,11,13,15},{16,18,20,22,24,26,28,30},{17..., dimensions={0} | all-to-all | bytes 262144 | tf_op jit(solution)/shard_map/all_to_all | solution.py:306
  52.5 0.0 collective-permute-start.5
  52.5 1.3 %collective-permute-done.5.other_ref = bf16[8,64,128]{2,1,0:T(8,128)(2,1)S(1)} collective-permute-done((bf16[8,64,128]{2,1,0:T(8,128)(2,1)S(1)}, bf16[8,64,128]{2,1,0:T(8,128)(2,1)S(1)}, u32[]{:S(2)}, u32[]{:S(2)}) %collective-permute-start.5) | collective-permute-done | bytes 131104 | tf_op jit(solution)/shard_map/ppermute | solution.py:307
  53.9 1.0 %decode.1 = f32[72,2,512]{2,1,0:T(2,128)} custom-call(s32[1]{0:T(128)} %bitcast.parity_ref, s32[72,128]{1,0:T(8,128)S(1)} %bitcast.21, f32[1,72]{1,0:T(1,128)S(1)} %bitcast.25, bf16[8,64,128]{2,1,0:T(8,128)(2,1)S(1)} %all_to_all.5.same_ref, bf16[8,64,128]{2,1,0:T(8,128)(2,1)S(1)} %collective-permute-done.5.other_ref), custom_call_target="tpu_custom_call" | custom-call | tf_op jit(solution)/shard_map/decode/pallas_call | solution.py:252
  (13 shorter events, 0.1 us)
Async XLA Ops:
  0.0 1.5 %copy-start.8 = (f32[72]{0:T(128)S(1)}, f32[72]{0:T(128)}, u32[]{:S(2)}) copy-start(f32[72]{0:T(128)} %param.8) | copy-start | bytes 868
  0.0 4.6 %copy-start = (bf16[3,72,8192]{2,1,0:T(8,128)(2,1)S(1)}, bf16[3,72,8192]{2,1,0:T(8,128)(2,1)}, u32[]{:S(2)}) copy-start(bf16[3,72,8192]{2,1,0:T(8,128)(2,1)} %influence.1) | copy-start | bytes 10616836
  2.4 0.6 %copy-start.2 = (bf16[72,128]{1,0:T(8,128)(2,1)}, bf16[72,128]{1,0:T(8,128)(2,1)S(1)}, u32[]{:S(2)}) copy-start(bf16[72,128]{1,0:T(8,128)(2,1)S(1)} %multiply_convert_fusion.cmds_ref) | copy-start | bytes 55300
  4.1 4.2 %collective-permute-start.1 = (bf16[72,8320]{1,0:T(8,128)(2,1)}, bf16[72,8320]{1,0:T(8,128)(2,1)}, u32[]{:S(2)}, u32[]{:S(2)}) collective-permute-start(bf16[72,8320]{1,0:T(8,128)(2,1)} %pad_maximum_fusion), channel_id=1, source_target_pairs={{0,1},{1,0},{2,3},{3,2},{4,5},{5,4},{6,7},{7,6},{8,9},{9,8},{10,11... | collective-permute-start | bytes 3594248 | tf_op jit(solution)/shard_map/ppermute | solution.py:294
  4.6 3.7 %copy-start.1 = (f32[512,256]{1,0:T(8,128)S(1)}, f32[512,256]{1,0:T(8,128)}, u32[]{:S(2)}) copy-start(f32[512,256]{1,0:T(8,128)} %constant.30.clone.table_ref) | copy-start | bytes 1572868
  4.6 3.7 %copy-start.3 = (bf16[72,128]{1,0:T(8,128)(2,1)S(1)}, bf16[72,128]{1,0:T(8,128)(2,1)}, u32[]{:S(2)}) copy-start(bf16[72,128]{1,0:T(8,128)(2,1)} %copy-done.2) | copy-start | bytes 55300
  4.6 3.8 %copy-start.5 = (f32[32,16,16]{0,2,1:T(8,128)S(1)}, f32[32,16,16]{0,2,1:T(8,128)}, u32[]{:S(2)}) copy-start(f32[32,16,16]{0,2,1:T(8,128)} %param.10) | copy-start | bytes 98308
  4.6 3.8 %copy-start.6 = (f32[32,16,16]{0,2,1:T(8,128)S(1)}, f32[32,16,16]{0,2,1:T(8,128)}, u32[]{:S(2)}) copy-start(f32[32,16,16]{0,2,1:T(8,128)} %param.11) | copy-start | bytes 98308
  5.5 9.0 %collective-permute-start = (bf16[72,3200]{1,0:T(8,128)(2,1)S(1)}, bf16[72,3200]{1,0:T(8,128)(2,1)S(1)}, u32[]{:S(2)}, u32[]{:S(2)}) collective-permute-start(bf16[72,3200]{1,0:T(8,128)(2,1)S(1)} %pad_maximum_fusion.1), channel_id=1, source_target_pairs={{1,2},{2,1},{3,4},{4,3},{5,6},{6,5},{7,8},{8,7},{9,10},{10,9},{11,... | collective-permute-start | bytes 1382408 | tf_op jit(solution)/shard_map/ppermute | solution.py:292
  6.3 12.1 %collective-permute-start.4 = (bf16[72,2048]{1,0:T(8,128)(2,1)S(1)}, bf16[72,2048]{1,0:T(8,128)(2,1)S(1)}, u32[]{:S(2)}, u32[]{:S(2)}) collective-permute-start(bf16[72,2048]{1,0:T(8,128)(2,1)S(1)} %get-tuple-element.13), channel_id=1, source_target_pairs={{1,2},{2,1},{3,4},{4,3},{5,6},{6,5},{7,8},{8,7},{9,10},{10,9},{11,... | collective-permute-start | bytes 884744 | tf_op jit(solution)/shard_map/ppermute | solution.py:292
  6.9 14.2 %collective-permute-start.3 = (bf16[72,2048]{1,0:T(8,128)(2,1)S(1)}, bf16[72,2048]{1,0:T(8,128)(2,1)S(1)}, u32[]{:S(2)}, u32[]{:S(2)}) collective-permute-start(bf16[72,2048]{1,0:T(8,128)(2,1)S(1)} %get-tuple-element.14), channel_id=1, source_target_pairs={{1,2},{2,1},{3,4},{4,3},{5,6},{6,5},{7,8},{8,7},{9,10},{10,9},{11,... | collective-permute-start | bytes 884744 | tf_op jit(solution)/shard_map/ppermute | solution.py:292
  7.7 16.2 %collective-permute-start.2 = (bf16[72,1024]{1,0:T(8,128)(2,1)S(1)}, bf16[72,1024]{1,0:T(8,128)(2,1)S(1)}, u32[]{:S(2)}, u32[]{:S(2)}) collective-permute-start(bf16[72,1024]{1,0:T(8,128)(2,1)S(1)} %dynamic-slice_bitcast_fusion.4), channel_id=1, source_target_pairs={{1,2},{2,1},{3,4},{4,3},{5,6},{6,5},{7,8},{8,7},{9,10},{10,9},{11,... | collective-permute-start | bytes 442376 | tf_op jit(solution)/shard_map/ppermute | solution.py:292
  8.4 6.1 %copy-start.7 = (s32[32]{0:T(128)S(1)}, s32[32]{0:T(128)}, u32[]{:S(2)}) copy-start(s32[32]{0:T(128)} %refs_0_.7) | copy-start | bytes 388
  23.8 30.0 %copy-start.4 = (s32[128,72]{0,1:T(8,128)S(1)}, s32[128,72]{0,1:T(8,128)}, u32[]{:S(2)}) copy-start(s32[128,72]{0,1:T(8,128)} %param.7) | copy-start | bytes 110596
  52.5 1.3 %collective-permute-start.5 = (bf16[8,64,128]{2,1,0:T(8,128)(2,1)S(1)}, bf16[8,64,128]{2,1,0:T(8,128)(2,1)S(1)}, u32[]{:S(2)}, u32[]{:S(2)}) collective-permute-start(bf16[8,64,128]{2,1,0:T(8,128)(2,1)S(1)} %all_to_all.5.same_ref), channel_id=1, source_target_pairs={{0,1},{1,0},{2,3},{3,2},{4,5},{5,4},{6,7},{7,6},{8,9},{9,8},{10,11... | collective-permute-start | bytes 393224 | tf_op jit(solution)/shard_map/ppermute | solution.py:307

commit v3 on v2

--- a/solution.py
+++ b/solution.py
@@ -25,7 +25,7 @@
     root = math.sqrt(2.0)
     return (
         power_fit(root * np.sin(np.pi * r) / r, nodes, 3),
-        power_fit(root * np.cos(np.pi * r), nodes, 4),
+        power_fit(root * np.cos(np.pi * r), nodes, 3),
     )
 
 
@@ -109,7 +109,7 @@
     whole = pl.BlockSpec(memory_space=pltpu.VMEM)
     return pl.pallas_call(
         prepare_kernel,
-        in_specs=[whole] * 5 + [pl.BlockSpec(memory_space=pl.ANY)],
+        in_specs=[whole] * 5 + [pl.BlockSpec(memory_space=pltpu.HBM)],
         out_specs=[whole] * 2,
         out_shape=[
             jax.ShapeDtypeStruct((subs, half, flat), jnp.bfloat16),
@@ -259,6 +259,85 @@
     )(parity.reshape(1), signs, stroke.reshape(1, acts), same, other)
 
 
+def in_hbm(value):
+    return pltpu.with_memory_space_constraint(value, pltpu.HBM)
+
+
+def pack_first_kernel(parity_ref, signs_hbm, stroke_hbm, influence, sent_ref, cmds_ref, signs, stroke, arrivals):
+    acts, patterns = cmds_ref.shape
+    width = sent_ref.shape[1] - patterns
+    moves = (
+        (signs_hbm, signs),
+        (stroke_hbm, stroke),
+        (influence.at[2 * parity_ref[0], :, pl.ds(0, width)], sent_ref.at[:, pl.ds(0, width)]),
+    )
+    fetches = [pltpu.make_async_copy(*move, arrivals.at[k]) for k, move in enumerate(moves)]
+    for fetch in fetches:
+        fetch.start()
+    fetches[0].wait()
+    fetches[1].wait()
+    column = jnp.broadcast_to(stroke[...][None, :], (LANES, acts)).T[:, :1]
+    commands = (column * signs[...].astype(jnp.float32)).astype(jnp.bfloat16)
+    cmds_ref[...] = commands
+    sent_ref[:, width:] = commands
+    fetches[2].wait()
+
+
+def pack_first(parity, signs, stroke, influence, width):
+    acts, patterns = signs.shape
+    whole, far_off = pl.BlockSpec(memory_space=pltpu.VMEM), pl.BlockSpec(memory_space=pltpu.HBM)
+    return pl.pallas_call(
+        pack_first_kernel,
+        in_specs=[pl.BlockSpec(memory_space=pltpu.SMEM)] + [far_off] * 3,
+        out_specs=[whole] * 2,
+        out_shape=[
+            jax.ShapeDtypeStruct((acts, width + patterns), jnp.bfloat16),
+            jax.ShapeDtypeStruct((acts, patterns), jnp.bfloat16),
+        ],
+        scratch_shapes=[
+            pltpu.VMEM((acts, patterns), jnp.int32),
+            pltpu.VMEM((acts,), jnp.float32),
+            pltpu.SemaphoreType.DMA((3,)),
+        ],
+        compiler_params=pltpu.CompilerParams(vmem_limit_bytes=8 << 20),
+        name="pack_first",
+    )(parity.reshape(1), signs, stroke, influence)
+
+
+def pack_rest_kernel(parity_ref, cmds_ref, influence, *refs):
+    pieces, near_ref, arrivals = refs[:-2], refs[-2], refs[-1]
+    points = influence.shape[2]
+    far_row, near_row = 2 * parity_ref[0], 2 - 2 * parity_ref[0]
+    fetches = [
+        pltpu.make_async_copy(influence.at[near_row], near_ref.at[:, pl.ds(0, points)], arrivals.at[0])
+    ]
+    first = points - sum(ref.shape[1] for ref in pieces)
+    for k, ref in enumerate(pieces):
+        source = influence.at[far_row, :, pl.ds(first, ref.shape[1])]
+        fetches.append(pltpu.make_async_copy(source, ref, arrivals.at[k + 1]))
+        first += ref.shape[1]
+    for fetch in fetches:
+        fetch.start()
+    near_ref[:, points:] = cmds_ref[...]
+    for fetch in fetches:
+        fetch.wait()
+
+
+def pack_rest(parity, commands, influence, widths):
+    acts, patterns = commands.shape
+    whole = pl.BlockSpec(memory_space=pltpu.VMEM)
+    shapes = [(acts, width) for width in widths] + [(acts, influence.shape[2] + patterns)]
+    return pl.pallas_call(
+        pack_rest_kernel,
+        in_specs=[pl.BlockSpec(memory_space=pltpu.SMEM), whole, pl.BlockSpec(memory_space=pltpu.HBM)],
+        out_specs=[whole] * len(shapes),
+        out_shape=[jax.ShapeDtypeStruct(shape, jnp.bfloat16) for shape in shapes],
+        scratch_shapes=[pltpu.SemaphoreType.DMA((len(shapes),))],
+        compiler_params=pltpu.CompilerParams(vmem_limit_bytes=8 << 20),
+        name="pack_rest",
+    )(parity.reshape(1), commands, influence)
+
+
 def pairings(count):
     near = [(i, i ^ 1) for i in range(count) if (i ^ 1) < count]
     far = [(i, i + 1 if i % 2 else i - 1) for i in range(count)]
@@ -267,35 +346,29 @@
 
 def chunk_sizes(subs):
     unit = subs // 8
-    return [3 * unit, 2 * unit, 2 * unit, unit]
+    return [k * unit for k in (2, 2, 2, 2)]
 
 
 def interaction(hadamard, stroke, influence, amplitude, aberration, valid_mask):
     count = lax.axis_size("tile")
     parity = lax.axis_index("tile") % 2
-    acts = stroke.shape[0]
     subs = amplitude.shape[0]
     flat = influence.shape[2] // subs
     near, far = pairings(count)
+    influence = in_hbm(influence)
     sizes = chunk_sizes(subs)
     firsts = [sum(sizes[:k]) for k in range(len(sizes))]
-    commands = (stroke[:, None] * hadamard.T.astype(jnp.float32)).astype(jnp.bfloat16)
-
-    def slab_of(offset, first, size):
-        return lax.dynamic_slice(influence, (offset, 0, first * flat), (1, acts, size * flat))[0]
-
-    far_slabs = []
-    for k, (first, size) in enumerate(zip(firsts, sizes)):
-        sent = slab_of(2 * parity, first, size)
-        if k == 0:
-            sent = jnp.concatenate([sent, commands], axis=1)
-        far_slabs.append(lax.ppermute(sent, "tile", far))
-    sent = jnp.concatenate([slab_of(2 - 2 * parity, 0, subs), commands], axis=1)
-    near_sent = lax.ppermute(sent, "tile", near)
+    widths = [size * flat for size in sizes]
+    first_sent, commands = pack_first(parity, in_hbm(hadamard.T), in_hbm(stroke), influence, widths[0])
+    far_slabs = [lax.ppermute(first_sent, "tile", far)]
+    *rest, near_slab = pack_rest(parity, commands, influence, widths[1:])
+    near_sent = lax.ppermute(near_slab, "tile", near)
+    for piece in rest:
+        far_slabs.append(lax.ppermute(piece, "tile", far))
     transform, phase = prepare(commands, near_sent, influence, amplitude, aberration)
     parts, far_cmds = [], None
     for k, (first, size) in enumerate(zip(firsts, sizes)):
-        earlier = parts if k == len(sizes) - 1 else []
+        earlier = parts[-1:]
         found = spot_slopes(valid_mask, far_cmds, far_slabs[k], transform, phase, first, size, earlier)
         parts.append(found[0])
         if k == 0:

time: 55.1 us -> 52.4 us (0.951)
  other arithmetic: 2.81 us -> 0 us
  local copies, waits for them, and re-layouts: 2.26 us -> 0.05 us
  blocking collectives: 27 us -> 28.3 us
  Pallas kernels: 18 us -> 18.9 us
    pallas_call x0 -> x2, Pallas kernels: none -> 2.63 us  [the longest x1 1.54 us: pack_rest(): pl.pallas_call(pack_rest_kernel, in_specs=[pl.BlockSpec(memory_space=pltp...]
    concatenate x2 -> x0, other arithmetic: 1.97 us -> none  [the longest x1 1.15 us: interaction(): sent = jnp.concatenate([slab_of(2 - 2 * parity, 0, subs), commands], axis=1)]
    squeeze x4 -> x0, local copies, waits for them, and re-layouts: 1.6 us -> none  [slab_of(): lax.dynamic_slice(influence, (offset, 0, first * flat), (1, acts, size *...]
    pallas_call x1, Pallas kernels: 6.08 us -> 4.57 us  [prepare(): pl.pallas_call(prepare_kernel, in_specs=[whole] * 5 + [pl.BlockSpec(memor...]
    all_to_all x1, blocking collectives: 27 us -> 28.3 us  [interaction(): same = lax.all_to_all(copies, 'tile', 0, 0, axis_index_groups=groups)]
    convert_element_type x1 -> x0, other arithmetic: 0.85 us -> none  [interaction(): (stroke[:, None] * hadamard.T.astype(jnp.float32)).astype(jnp.bfloat16)]
    unnamed x18 -> x12, local copies, waits for them, and re-layouts: 0.64 us -> 0.03 us
  transfers between devices with their start and end apart: 6 -> 6, of which waited for: 1 -> 1; matrix products, arithmetic and copies ran while one was open for 2% -> 0% of each run, Pallas kernels for 28% -> 24%
where the time goes in v3:
time: 52.4 us; the launch traced here: 52.1 us
  blocking collectives  28.3 us (54%)
  Pallas kernels  18.9 us (36%)
  starting transfers between devices  3.27 us (6%)
  waiting for transfers between devices  1.36 us (3%)
    all_to_all x1, blocking collectives, interaction(): same = lax.all_to_all(copies, 'tile', 0, 0, axis_index_groups=groups)  28.3 us
    pallas_call x4, Pallas kernels, spot_slopes(): pl.pallas_call(lambda *refs: spots_kernel(first, lead, len(earlier), *ref...  10.7 us
    pallas_call x1, Pallas kernels, prepare(): pl.pallas_call(prepare_kernel, in_specs=[whole] * 5 + [pl.BlockSpec(memor...  4.57 us
    ppermute x3, starting transfers between devices, interaction(): far_slabs.append(lax.ppermute(piece, 'tile', far))  2.04 us
    pallas_call x1, Pallas kernels, pack_rest(): pl.pallas_call(pack_rest_kernel, in_specs=[pl.BlockSpec(memory_space=pltp...  1.54 us
    ppermute x1, waiting for transfers between devices, interaction(): other = lax.ppermute(same, 'tile', near)  1.35 us
    pallas_call x1, Pallas kernels, pack_first(): pl.pallas_call(pack_first_kernel, in_specs=[pl.BlockSpec(memory_space=plt...  1.1 us
  transfers between devices with their start and end apart: 6, of which 1 were waited for; matrix products, arithmetic and copies ran while one was open for 0% of the time, Pallas kernels for 24%

profile of v3, /device:TPU:0, one launch (start us, length us, event | category | flops | bytes accessed | tf_op | source)
XLA Modules:
  0.0 52.1 jit_solution(17282158281337131766)
XLA Ops:
  0.0 0.0 copy-start
  0.0 0.0 copy-start.2
  0.0 1.1 %pack_first.1 = (bf16[72,2176]{1,0:T(8,128)(2,1)S(1)}, bf16[72,128]{1,0:T(8,128)(2,1)S(1)}) custom-call(s32[1]{0:T(128)} %bitcast.parity_ref, s32[72,128]{1,0:T(8,128)} %bitcast.10, f32[72]{0:T(128)} %stroke_hbm.1, bf16[3,72,8192]{2,1,0:T(8,128)(2,1)} %influence.5), custom_call_target="tpu_custom_call" | custom-call | tf_op jit(solution)/shard_map/pack_first/pallas_call | solution.py:289
  1.1 1.5 %pack_rest.1 = (bf16[72,2048]{1,0:T(8,128)(2,1)S(1)}, bf16[72,2048]{1,0:T(8,128)(2,1)S(1)}, bf16[72,2048]{1,0:T(8,128)(2,1)S(1)}, bf16[72,8320]{1,0:T(8,128)(2,1)S(1)}) custom-call(s32[1]{0:T(128)} %bitcast.parity_ref, bf16[72,128]{1,0:T(8,128)(2,1)S(1)} %get-tuple-element.16.cmds_ref, bf16[3,72,8192]{2,1,0:T(8,128)(2,1)} %influence.5), custom_call_target="tpu_custom_call" | custom-call | tf_op jit(solution)/shard_map/pack_rest/pallas_call | solution.py:330
  2.7 0.0 copy-start.4
  2.7 0.6 %collective-permute-start.1 = (bf16[72,8320]{1,0:T(8,128)(2,1)S(1)}, bf16[72,8320]{1,0:T(8,128)(2,1)S(1)}, u32[]{:S(2)}, u32[]{:S(2)}) collective-permute-start(bf16[72,8320]{1,0:T(8,128)(2,1)S(1)} %get-tuple-element.17), channel_id=1, source_target_pairs={{0,1},{1,0},{2,3},{3,2},{4,5},{5,4},{6,7},{7,6},{8,9},{9,8},{10,11... | collective-permute-start | bytes 3594248 | tf_op jit(solution)/shard_map/ppermute | solution.py:365
  3.2 0.7 %collective-permute-start = (bf16[72,2176]{1,0:T(8,128)(2,1)S(1)}, bf16[72,2176]{1,0:T(8,128)(2,1)S(1)}, u32[]{:S(2)}, u32[]{:S(2)}) collective-permute-start(bf16[72,2176]{1,0:T(8,128)(2,1)S(1)} %get-tuple-element.15), channel_id=1, source_target_pairs={{1,2},{2,1},{3,4},{4,3},{5,6},{6,5},{7,8},{8,7},{9,10},{10,9},{11,... | collective-permute-start | bytes 940040 | tf_op jit(solution)/shard_map/ppermute | solution.py:363
  3.9 0.7 %collective-permute-start.4 = (bf16[72,2048]{1,0:T(8,128)(2,1)S(1)}, bf16[72,2048]{1,0:T(8,128)(2,1)S(1)}, u32[]{:S(2)}, u32[]{:S(2)}) collective-permute-start(bf16[72,2048]{1,0:T(8,128)(2,1)S(1)} %get-tuple-element.23), channel_id=1, source_target_pairs={{1,2},{2,1},{3,4},{4,3},{5,6},{6,5},{7,8},{8,7},{9,10},{10,9},{11,... | collective-permute-start | bytes 884744 | tf_op jit(solution)/shard_map/ppermute | solution.py:367
  4.6 0.7 %collective-permute-start.3 = (bf16[72,2048]{1,0:T(8,128)(2,1)S(1)}, bf16[72,2048]{1,0:T(8,128)(2,1)S(1)}, u32[]{:S(2)}, u32[]{:S(2)}) collective-permute-start(bf16[72,2048]{1,0:T(8,128)(2,1)S(1)} %get-tuple-element.22), channel_id=1, source_target_pairs={{1,2},{2,1},{3,4},{4,3},{5,6},{6,5},{7,8},{8,7},{9,10},{10,9},{11,... | collective-permute-start | bytes 884744 | tf_op jit(solution)/shard_map/ppermute | solution.py:367
  5.3 0.7 %collective-permute-start.2 = (bf16[72,2048]{1,0:T(8,128)(2,1)S(1)}, bf16[72,2048]{1,0:T(8,128)(2,1)S(1)}, u32[]{:S(2)}, u32[]{:S(2)}) collective-permute-start(bf16[72,2048]{1,0:T(8,128)(2,1)S(1)} %get-tuple-element.21), channel_id=1, source_target_pairs={{1,2},{2,1},{3,4},{4,3},{5,6},{6,5},{7,8},{8,7},{9,10},{10,9},{11,... | collective-permute-start | bytes 884744 | tf_op jit(solution)/shard_map/ppermute | solution.py:367
  6.0 0.0 collective-permute-done.1.near_ref
  6.0 0.0 copy-done
  6.0 0.0 copy-done.2
  6.0 0.0 copy-done.3
  6.0 4.6 %prepare.1 = (bf16[32,512,256]{2,1,0:T(8,128)(2,1)S(1)}, f32[32,128,256]{2,1,0:T(8,128)S(1)}) custom-call(bf16[72,128]{1,0:T(8,128)(2,1)S(1)} %get-tuple-element.16.cmds_ref, bf16[72,8320]{1,0:T(8,128)(2,1)S(1)} %collective-permute-done.1.near_ref, f32[256,32]{1,0:T(8,128)S(1)} %bitcast.12, f32[256,32]{1,0:T(8,128)S(1)} %bitcast.13, f32[512,256]{1,0:T(8,128)S(1)} %copy-done, ...), custom_call_target="tpu_custom_call" | custom-call | flops 1000000000 | bytes 8388608 | tf_op jit(solution)/shard_map/prepare/pallas_call | solution.py:110
  10.6 0.0 collective-permute-done.refs_1_.refs_2_
  10.6 0.0 copy-done.4
  10.6 2.8 %spots.4 = (bf16[2,8,128]{2,1,0:T(8,128)(2,1)S(1)}, bf16[128,72]{1,0:T(8,128)(2,1)S(1)}) custom-call(s32[32]{0:T(128)S(1)} %copy-done.4, bf16[72,2176]{1,0:T(8,128)(2,1)S(1)} %collective-permute-done.refs_1_.refs_2_, bf16[72,2176]{1,0:T(8,128)(2,1)S(1)} %collective-permute-done.refs_1_.refs_2_, bf16[32,512,256]{2,1,0:T(8,128)(2,1)S(1)} %get-tuple-element.18.refs_3_, ...), custom_call_target="tpu_custom_call" | custom-call | flops 800000000 | bytes 1000000 | tf_op jit(solution)/shard_map/spots/pallas_call | solution.py:214
  13.4 0.0 collective-permute-done.4.refs_2_
  13.4 2.7 %spots.5.refs_5_ = bf16[2,16,128]{2,1,0:T(8,128)(2,1)S(1)} custom-call(s32[32]{0:T(128)S(1)} %copy-done.4, bf16[128,72]{1,0:T(8,128)(2,1)S(1)} %get-tuple-element.20.refs_1_, bf16[72,2048]{1,0:T(8,128)(2,1)S(1)} %collective-permute-done.4.refs_2_, bf16[32,512,256]{2,1,0:T(8,128)(2,1)S(1)} %get-tuple-element.18.refs_3_, ...), custom_call_target="tpu_custom_call" | custom-call | flops 800000000 | bytes 1000000 | tf_op jit(solution)/shard_map/spots/pallas_call | solution.py:214
  16.1 0.0 collective-permute-done.3.refs_2_
  16.1 2.7 %spots.6.refs_5_ = bf16[2,24,128]{2,1,0:T(8,128)(2,1)S(1)} custom-call(s32[32]{0:T(128)S(1)} %copy-done.4, bf16[128,72]{1,0:T(8,128)(2,1)S(1)} %get-tuple-element.20.refs_1_, bf16[72,2048]{1,0:T(8,128)(2,1)S(1)} %collective-permute-done.3.refs_2_, bf16[32,512,256]{2,1,0:T(8,128)(2,1)S(1)} %get-tuple-element.18.refs_3_, ...), custom_call_target="tpu_custom_call" | custom-call | flops 800000000 | bytes 1000000 | tf_op jit(solution)/shard_map/spots/pallas_call | solution.py:214
  18.7 0.0 copy-start.1
  18.7 0.0 copy-start.5
  18.8 0.0 collective-permute-done.2.refs_2_
  18.8 2.7 %spots.7 = bf16[2,32,128]{2,1,0:T(8,128)(2,1)S(1)} custom-call(s32[32]{0:T(128)S(1)} %copy-done.4, bf16[128,72]{1,0:T(8,128)(2,1)S(1)} %get-tuple-element.20.refs_1_, bf16[72,2048]{1,0:T(8,128)(2,1)S(1)} %collective-permute-done.2.refs_2_, bf16[32,512,256]{2,1,0:T(8,128)(2,1)S(1)} %get-tuple-element.18.refs_3_, ...), custom_call_target="tpu_custom_call" | custom-call | flops 800000000 | bytes 1000000 | tf_op jit(solution)/shard_map/spots/pallas_call | solution.py:214
  21.5 28.3 %all_to_all.5.same_ref = bf16[8,64,128]{2,1,0:T(8,128)(2,1)S(1)} all-to-all(bf16[8,64,128]{2,1,0:T(8,128)(2,1)S(1)} %broadcast_in_dim.3), channel_id=1, replica_groups={{0,2,4,6,8,10,12,14},{1,3,5,7,9,11,13,15},{16,18,20,22,24,26,28,30},{17..., dimensions={0} | all-to-all | bytes 262144 | tf_op jit(solution)/shard_map/all_to_all | solution.py:379
  49.8 0.0 collective-permute-start.5
  49.8 1.3 %collective-permute-done.5.other_ref = bf16[8,64,128]{2,1,0:T(8,128)(2,1)S(1)} collective-permute-done((bf16[8,64,128]{2,1,0:T(8,128)(2,1)S(1)}, bf16[8,64,128]{2,1,0:T(8,128)(2,1)S(1)}, u32[]{:S(2)}, u32[]{:S(2)}) %collective-permute-start.5) | collective-permute-done | bytes 131104 | tf_op jit(solution)/shard_map/ppermute | solution.py:380
  51.1 0.0 copy-done.1
  51.1 0.0 copy-done.5
  51.1 1.0 %decode.1 = f32[72,2,512]{2,1,0:T(2,128)} custom-call(s32[1]{0:T(128)} %bitcast.parity_ref, s32[72,128]{1,0:T(8,128)S(1)} %bitcast.11, f32[1,72]{1,0:T(1,128)S(1)} %bitcast.15, bf16[8,64,128]{2,1,0:T(8,128)(2,1)S(1)} %all_to_all.5.same_ref, bf16[8,64,128]{2,1,0:T(8,128)(2,1)S(1)} %collective-permute-done.5.other_ref), custom_call_target="tpu_custom_call" | custom-call | tf_op jit(solution)/shard_map/decode/pallas_call | solution.py:252
  (2 shorter events, 0.0 us)
Async XLA Ops:
  0.0 6.0 %copy-start = (f32[512,256]{1,0:T(8,128)S(1)}, f32[512,256]{1,0:T(8,128)}, u32[]{:S(2)}) copy-start(f32[512,256]{1,0:T(8,128)} %constant.19.clone.table_ref) | copy-start | bytes 1572868
  0.0 6.0 %copy-start.2 = (f32[32,16,16]{0,2,1:T(8,128)S(1)}, f32[32,16,16]{0,2,1:T(8,128)}, u32[]{:S(2)}) copy-start(f32[32,16,16]{0,2,1:T(8,128)} %param.10) | copy-start | bytes 98308
  0.0 6.0 %copy-start.3 = (f32[32,16,16]{0,2,1:T(8,128)S(1)}, f32[32,16,16]{0,2,1:T(8,128)}, u32[]{:S(2)}) copy-start(f32[32,16,16]{0,2,1:T(8,128)} %param.11) | copy-start | bytes 98308
  2.7 7.9 %copy-start.4 = (s32[32]{0:T(128)S(1)}, s32[32]{0:T(128)}, u32[]{:S(2)}) copy-start(s32[32]{0:T(128)} %refs_0_.7) | copy-start | bytes 388
  2.7 3.3 %collective-permute-start.1 = (bf16[72,8320]{1,0:T(8,128)(2,1)S(1)}, bf16[72,8320]{1,0:T(8,128)(2,1)S(1)}, u32[]{:S(2)}, u32[]{:S(2)}) collective-permute-start(bf16[72,8320]{1,0:T(8,128)(2,1)S(1)} %get-tuple-element.17), channel_id=1, source_target_pairs={{0,1},{1,0},{2,3},{3,2},{4,5},{5,4},{6,7},{7,6},{8,9},{9,8},{10,11... | collective-permute-start | bytes 3594248 | tf_op jit(solution)/shard_map/ppermute | solution.py:365
  3.2 7.4 %collective-permute-start = (bf16[72,2176]{1,0:T(8,128)(2,1)S(1)}, bf16[72,2176]{1,0:T(8,128)(2,1)S(1)}, u32[]{:S(2)}, u32[]{:S(2)}) collective-permute-start(bf16[72,2176]{1,0:T(8,128)(2,1)S(1)} %get-tuple-element.15), channel_id=1, source_target_pairs={{1,2},{2,1},{3,4},{4,3},{5,6},{6,5},{7,8},{8,7},{9,10},{10,9},{11,... | collective-permute-start | bytes 940040 | tf_op jit(solution)/shard_map/ppermute | solution.py:363
  3.9 9.5 %collective-permute-start.4 = (bf16[72,2048]{1,0:T(8,128)(2,1)S(1)}, bf16[72,2048]{1,0:T(8,128)(2,1)S(1)}, u32[]{:S(2)}, u32[]{:S(2)}) collective-permute-start(bf16[72,2048]{1,0:T(8,128)(2,1)S(1)} %get-tuple-element.23), channel_id=1, source_target_pairs={{1,2},{2,1},{3,4},{4,3},{5,6},{6,5},{7,8},{8,7},{9,10},{10,9},{11,... | collective-permute-start | bytes 884744 | tf_op jit(solution)/shard_map/ppermute | solution.py:367
  4.6 11.5 %collective-permute-start.3 = (bf16[72,2048]{1,0:T(8,128)(2,1)S(1)}, bf16[72,2048]{1,0:T(8,128)(2,1)S(1)}, u32[]{:S(2)}, u32[]{:S(2)}) collective-permute-start(bf16[72,2048]{1,0:T(8,128)(2,1)S(1)} %get-tuple-element.22), channel_id=1, source_target_pairs={{1,2},{2,1},{3,4},{4,3},{5,6},{6,5},{7,8},{8,7},{9,10},{10,9},{11,... | collective-permute-start | bytes 884744 | tf_op jit(solution)/shard_map/ppermute | solution.py:367
  5.3 13.5 %collective-permute-start.2 = (bf16[72,2048]{1,0:T(8,128)(2,1)S(1)}, bf16[72,2048]{1,0:T(8,128)(2,1)S(1)}, u32[]{:S(2)}, u32[]{:S(2)}) collective-permute-start(bf16[72,2048]{1,0:T(8,128)(2,1)S(1)} %get-tuple-element.21), channel_id=1, source_target_pairs={{1,2},{2,1},{3,4},{4,3},{5,6},{6,5},{7,8},{8,7},{9,10},{10,9},{11,... | collective-permute-start | bytes 884744 | tf_op jit(solution)/shard_map/ppermute | solution.py:367
  18.7 32.4 %copy-start.1 = (s32[128,72]{0,1:T(8,128)S(1)}, s32[128,72]{0,1:T(8,128)}, u32[]{:S(2)}) copy-start(s32[128,72]{0,1:T(8,128)} %param.7) | copy-start | bytes 110596
  18.7 32.4 %copy-start.5 = (f32[72]{0:T(128)S(1)}, f32[72]{0:T(128)}, u32[]{:S(2)}) copy-start(f32[72]{0:T(128)} %stroke_hbm.1) | copy-start | bytes 868
  49.8 1.3 %collective-permute-start.5 = (bf16[8,64,128]{2,1,0:T(8,128)(2,1)S(1)}, bf16[8,64,128]{2,1,0:T(8,128)(2,1)S(1)}, u32[]{:S(2)}, u32[]{:S(2)}) collective-permute-start(bf16[8,64,128]{2,1,0:T(8,128)(2,1)S(1)} %all_to_all.5.same_ref), channel_id=1, source_target_pairs={{0,1},{1,0},{2,3},{3,2},{4,5},{5,4},{6,7},{7,6},{8,9},{9,8},{10,11... | collective-permute-start | bytes 393224 | tf_op jit(solution)/shard_map/ppermute | solution.py:380

commit v4 on v3

v4 whole, which is shorter than its diff:
```python
import math

import jax
import jax.numpy as jnp
import numpy as np
from jax import lax
from jax.experimental import pallas as pl
from jax.experimental.pallas import tpu as pltpu
from jax.sharding import PartitionSpec as P


PIX = 16
LANES = 8
GROUP = 8
ROWS = 16


def power_fit(values, nodes, degree):
    fit = np.polynomial.chebyshev.Chebyshev.fit(nodes, values, degree, domain=[0, 0.25])
    return [float(c) for c in fit.convert(kind=np.polynomial.Polynomial).coef]


def half_turn_fits():
    nodes = 0.125 * (1.0 - np.cos(np.pi * (np.arange(200) + 0.5) / 200))
    r = np.sqrt(nodes)
    root = math.sqrt(2.0)
    return (
        power_fit(root * np.sin(np.pi * r) / r, nodes, 3),
        power_fit(root * np.cos(np.pi * r), nodes, 3),
    )


SIN_FIT, COS_FIT = half_turn_fits()


def horner(coefs, z):
    value = z * coefs[-1] + coefs[-2]
    for c in coefs[-3::-1]:
        value = value * z + c
    return value


def cos_sin(phase):
    turns = phase * (1.0 / (2.0 * math.pi))
    r = turns - jnp.round(turns)
    z = r * r
    half_sin = horner(SIN_FIT, z) * r
    half_cos = horner(COS_FIT, z)
    return 1.0 - half_sin * half_sin, half_sin * half_cos


def dft_table(samples, pixels):
    freqs = np.arange(pixels) - pixels / 2.0
    table = np.exp(-2j * np.pi * freqs[:, None] * np.arange(samples)[None, :] / (2.0 * samples))
    full = np.kron(table, table)
    return np.concatenate([full.real, full.imag]).astype(np.float32)


def bf16_term(commands, slab):
    term = jnp.dot(commands, slab, preferred_element_type=jnp.float32)
    return term.astype(jnp.bfloat16).astype(jnp.float32)


def turned(ref_value):
    return ref_value.astype(jnp.float32).T.astype(jnp.bfloat16)


def prepare_kernel(
    mask_ref, cmds_ref, near_ref, amp_ref, abe_ref, table_ref, influence, trans_ref, phase_ref, valid_ref, field, own_slab, cmds, arrival
):
    subs, flat = trans_ref.shape[0], trans_ref.shape[2]
    half = trans_ref.shape[1] // 2
    fetch = pltpu.make_async_copy(influence.at[1], own_slab, arrival)
    fetch.start()
    cosine, sine = cos_sin(abe_ref[...])
    field[0] = (amp_ref[...] * cosine).T
    field[1] = (amp_ref[...] * sine).T
    row = lax.broadcasted_iota(jnp.int32, valid_ref.shape, 0)
    valid = jnp.zeros(valid_ref.shape, jnp.float32)
    for s in range(subs):
        valid = jnp.where(row == s, mask_ref[s].astype(jnp.float32), valid)
    valid_ref[...] = valid
    cmds[0] = turned(cmds_ref[...])
    cmds[1] = turned(near_ref[:, subs * flat :])

    def fold(s, carry):
        real, imag = field[0, pl.ds(s, 1), :], field[1, pl.ds(s, 1), :]
        real = jnp.broadcast_to(real, (PIX, flat))
        imag = jnp.broadcast_to(imag, (PIX, flat))
        for row in range(0, half, PIX):
            upper, lower = table_ref[row : row + PIX], table_ref[half + row : half + row + PIX]
            trans_ref[s, 2 * row : 2 * row + PIX] = (upper * real - lower * imag).astype(jnp.bfloat16)
            trans_ref[s, 2 * row + PIX : 2 * row + 2 * PIX] = (lower * real + upper * imag).astype(jnp.bfloat16)
        return carry

    lax.fori_loop(0, subs, fold, 0)
    fetch.wait()

    def add_terms(g, carry):
        for k in range(GROUP):
            s = g * GROUP + k
            cols = pl.ds(pl.multiple_of(s * flat, flat), flat)
            phase_ref[s] = bf16_term(cmds[0], own_slab[:, cols]) + bf16_term(cmds[1], near_ref[:, cols])
        return carry

    lax.fori_loop(0, subs // GROUP, add_terms, 0)


def prepare(mask, commands, near_sent, influence, amplitude, aberration):
    subs, samples = amplitude.shape[0], amplitude.shape[1]
    flat = samples * samples
    acts, patterns = commands.shape
    table = jnp.asarray(dft_table(samples, PIX))
    half = table.shape[0]
    whole = pl.BlockSpec(memory_space=pltpu.VMEM)
    return pl.pallas_call(
        prepare_kernel,
        in_specs=[pl.BlockSpec(memory_space=pltpu.SMEM)] + [whole] * 5 + [pl.BlockSpec(memory_space=pltpu.HBM)],
        out_specs=[whole] * 3,
        out_shape=[
            jax.ShapeDtypeStruct((subs, half, flat), jnp.bfloat16),
            jax.ShapeDtypeStruct((subs, patterns, flat), jnp.float32),
            jax.ShapeDtypeStruct((subs, patterns), jnp.float32),
        ],
        scratch_shapes=[
            pltpu.VMEM((2, subs, flat), jnp.float32),
            pltpu.VMEM((acts, subs * flat), jnp.bfloat16),
            pltpu.VMEM((2, patterns, acts), jnp.bfloat16),
            pltpu.SemaphoreType.DMA,
        ],
        compiler_params=pltpu.CompilerParams(vmem_limit_bytes=8 << 20),
        cost_estimate=pl.CostEstimate(flops=10**9, bytes_accessed=8 << 20, transcendentals=0),
        name="prepare",
    )(
        mask,
        commands,
        near_sent,
        amplitude.reshape(subs, flat).T,
        aberration.reshape(subs, flat).T,
        table,
        influence,
    )


def advance(running, pairs):
    (even_low, odd_low), (even_high, odd_high) = pairs
    if running is None:
        return (even_low, even_high, None), (odd_low, odd_high, None)
    found = []
    for (low, high, steps), more_low, more_high in zip(running, (even_low, odd_low), (even_high, odd_high)):
        both = low + high
        found.append((low + more_low, high + more_high, both if steps is None else steps + both))
    return found


def moments_of(low, high, steps):
    middle = (PIX - 1) / 2.0
    total = low + high
    row = lax.broadcasted_iota(jnp.int32, total.shape, 0).astype(jnp.float32)
    return total, total * middle - steps, low * (row - middle) + high * (row + (LANES - middle))


def spots_kernel(first, lead, done, valid_ref, cmds_ref, slab_ref, trans_ref, phase_ref, *refs):
    earlier, refs = refs[:done], refs[done:]
    out_ref, refs = refs[0], refs[1:]
    sums = refs[-1]
    flat = trans_ref.shape[2]
    patterns = out_ref.shape[2]
    count = sums.shape[2]
    size = math.gcd(count, GROUP)
    if lead:
        cmds = refs[0]
        cmds[...] = turned(cmds_ref[:, count * flat :])
    else:
        cmds = cmds_ref

    def group(g, carry):
        for k in range(size):
            s = g * size + k
            cols = pl.ds(pl.multiple_of(s * flat, flat), flat)
            term = jnp.dot(cmds[...], slab_ref[:, cols], preferred_element_type=jnp.float32)
            pieces = []
            for row in range(0, patterns, ROWS):
                part = term[row : row + ROWS].astype(jnp.bfloat16).astype(jnp.float32)
                phase = phase_ref[first + s, row : row + ROWS] + part
                pieces.append([w.astype(jnp.bfloat16) for w in cos_sin(phase)])
            waves = jnp.concatenate([p[0] for p in pieces] + [p[1] for p in pieces], axis=0)
            focal = lax.dot_general(
                trans_ref[first + s],
                waves,
                (((1,), (1,)), ((), ())),
                preferred_element_type=jnp.float32,
            )
            lines = focal.reshape(PIX, 2, PIX // LANES, LANES, 2 * patterns)
            running = None
            for u in range(PIX):
                pairs = []
                for v in range(PIX // LANES):
                    ur, vr = lines[u, 0, v, :, :patterns], lines[u, 0, v, :, patterns:]
                    ui, vi = lines[u, 1, v, :, :patterns], lines[u, 1, v, :, patterns:]
                    pairs.append(((ur * ur + ui * ui) + (vr * vr + vi * vi), ui * vr - ur * vi))
                running = advance(running, pairs)
            for kind, state in enumerate(running):
                for m, value in enumerate(moments_of(*state)):
                    sums[kind, m, s] = value
        return carry

    lax.fori_loop(0, count // size, group, 0)
    total = jnp.sum(sums[...], axis=3)
    even, odd = total[0], 2.0 * total[1]
    scale = 1.0 / ((even[0] + odd[0]) * (even[0] - odd[0]))
    scale = scale * valid_ref[first : first + count]
    for c in range(2):
        slope = ((odd[1 + c] * even[0] - even[1 + c] * odd[0]) * scale).astype(out_ref.dtype)
        pieces = [ref[c] for ref in earlier] + [slope]
        out_ref[c] = jnp.concatenate(pieces, axis=0) if earlier else slope


def spot_slopes(valid, cmds, slab, transform, phase, first, count, earlier):
    acts = slab.shape[0]
    patterns = phase.shape[1]
    lead = cmds is None
    rows = count + sum(part.shape[1] for part in earlier)
    whole = pl.BlockSpec(memory_space=pltpu.VMEM)
    out_shape = [jax.ShapeDtypeStruct((2, rows, patterns), jnp.bfloat16)]
    if lead:
        out_shape.append(jax.ShapeDtypeStruct((patterns, acts), jnp.bfloat16))
    return pl.pallas_call(
        lambda *refs: spots_kernel(first, lead, len(earlier), *refs),
        in_specs=[whole] * (5 + len(earlier)),
        out_specs=[whole] * len(out_shape),
        out_shape=out_shape,
        scratch_shapes=[pltpu.VMEM((2, 3, count, LANES, patterns), jnp.float32)],
        compiler_params=pltpu.CompilerParams(vmem_limit_bytes=8 << 20),
        cost_estimate=pl.CostEstimate(flops=10**8 * count, bytes_accessed=10**6, transcendentals=0),
        name="spots",
    )(valid, slab if lead else cmds, slab, transform, phase, *earlier)


def decode_kernel(signs_ref, stroke_ref, same_ref, other_ref, out_ref):
    pairs, rows, patterns = same_ref.shape
    acts = signs_ref.shape[0]
    subs = rows // 2
    signs = signs_ref[...].astype(jnp.float32).astype(jnp.bfloat16)
    scale = jnp.broadcast_to(1.0 / (stroke_ref[...] * patterns), (LANES, acts)).T[:, :1]

    def write(even_ref, odd_ref):
        for c in range(2):
            part = slice(c * subs, (c + 1) * subs)
            slopes = jnp.stack([even_ref[:, part, :], odd_ref[:, part, :]], axis=1)
            summed = lax.dot_general(
                signs,
                slopes.reshape(2 * pairs * subs, patterns),
                (((1,), (1,)), ((), ())),
                preferred_element_type=jnp.float32,
            )
            out_ref[:, c, :] = summed * scale

    parity = tile_parity()
    pl.when(parity == 0)(lambda: write(same_ref, other_ref))
    pl.when(parity == 1)(lambda: write(other_ref, same_ref))


def decode(signs, stroke, same, other):
    pairs, rows, _ = same.shape
    acts = signs.shape[0]
    return pl.pallas_call(
        decode_kernel,
        in_specs=[pl.BlockSpec(memory_space=pltpu.VMEM)] * 4,
        out_specs=pl.BlockSpec(memory_space=pltpu.VMEM),
        out_shape=jax.ShapeDtypeStruct((acts, 2, pairs * rows), jnp.float32),
        compiler_params=pltpu.CompilerParams(vmem_limit_bytes=8 << 20),
        name="decode",
    )(signs, stroke.reshape(1, acts), same, other)


def tile_parity():
    return lax.rem(lax.axis_index("tile"), 2)


def in_hbm(value):
    return pltpu.with_memory_space_constraint(value, pltpu.HBM)


def pack_first_kernel(signs_hbm, stroke_hbm, influence, sent_ref, cmds_ref, signs, stroke, arrivals):
    acts, patterns = cmds_ref.shape
    width = sent_ref.shape[1] - patterns
    far_row = 2 * tile_parity()
    moves = (
        (signs_hbm, signs),
        (stroke_hbm, stroke),
        (influence.at[far_row, :, pl.ds(0, width)], sent_ref.at[:, pl.ds(0, width)]),
    )
    fetches = [pltpu.make_async_copy(*move, arrivals.at[k]) for k, move in enumerate(moves)]
    for fetch in fetches:
        fetch.start()
    fetches[0].wait()
    fetches[1].wait()
    column = jnp.broadcast_to(stroke[...][None, :], (LANES, acts)).T[:, :1]
    commands = (column * signs[...].astype(jnp.float32)).astype(jnp.bfloat16)
    cmds_ref[...] = commands
    sent_ref[:, width:] = commands
    fetches[2].wait()


def pack_first(signs, stroke, influence, width):
    acts, patterns = signs.shape
    whole, far_off = pl.BlockSpec(memory_space=pltpu.VMEM), pl.BlockSpec(memory_space=pltpu.HBM)
    return pl.pallas_call(
        pack_first_kernel,
        in_specs=[far_off] * 3,
        out_specs=[whole] * 2,
        out_shape=[
            jax.ShapeDtypeStruct((acts, width + patterns), jnp.bfloat16),
            jax.ShapeDtypeStruct((acts, patterns), jnp.bfloat16),
        ],
        scratch_shapes=[
            pltpu.VMEM((acts, patterns), jnp.int32),
            pltpu.VMEM((acts,), jnp.float32),
            pltpu.SemaphoreType.DMA((3,)),
        ],
        compiler_params=pltpu.CompilerParams(vmem_limit_bytes=8 << 20),
        name="pack_first",
    )(signs, stroke, influence)


def pack_rest_kernel(cmds_ref, influence, *refs):
    pieces, near_ref, arrivals = refs[:-2], refs[-2], refs[-1]
    points = influence.shape[2]
    far_row = 2 * tile_parity()
    near_row = 2 - far_row
    fetches = [
        pltpu.make_async_copy(influence.at[near_row], near_ref.at[:, pl.ds(0, points)], arrivals.at[0])
    ]
    first = points - sum(ref.shape[1] for ref in pieces)
    for k, ref in enumerate(pieces):
        source = influence.at[far_row, :, pl.ds(first, ref.shape[1])]
        fetches.append(pltpu.make_async_copy(source, ref, arrivals.at[k + 1]))
        first += ref.shape[1]
    for fetch in fetches:
        fetch.start()
    near_ref[:, points:] = cmds_ref[...]
    for fetch in fetches:
        fetch.wait()


def pack_rest(commands, influence, widths):
    acts, patterns = commands.shape
    whole = pl.BlockSpec(memory_space=pltpu.VMEM)
    shapes = [(acts, width) for width in widths] + [(acts, influence.shape[2] + patterns)]
    return pl.pallas_call(
        pack_rest_kernel,
        in_specs=[whole, pl.BlockSpec(memory_space=pltpu.HBM)],
        out_specs=[whole] * len(shapes),
        out_shape=[jax.ShapeDtypeStruct(shape, jnp.bfloat16) for shape in shapes],
        scratch_shapes=[pltpu.SemaphoreType.DMA((len(shapes),))],
        compiler_params=pltpu.CompilerParams(vmem_limit_bytes=8 << 20),
        name="pack_rest",
    )(commands, influence)


def pairings(count):
    near = [(i, i ^ 1) for i in range(count) if (i ^ 1) < count]
    far = [(i, i + 1 if i % 2 else i - 1) for i in range(count)]
    return near, [(a, b) for a, b in far if 0 <= b < count]


def chunk_sizes(subs):
    unit = subs // 8
    return [k * unit for k in (2, 2, 2, 1, 1)]


def interaction(hadamard, stroke, influence, amplitude, aberration, valid_mask):
    count = lax.axis_size("tile")
    subs = amplitude.shape[0]
    flat = influence.shape[2] // subs
    near, far = pairings(count)
    influence = in_hbm(influence)
    sizes = chunk_sizes(subs)
    firsts = [sum(sizes[:k]) for k in range(len(sizes))]
    widths = [size * flat for size in sizes]
    first_sent, commands = pack_first(in_hbm(hadamard.T), in_hbm(stroke), influence, widths[0])
    far_slabs = [lax.ppermute(first_sent, "tile", far)]
    *rest, near_slab = pack_rest(commands, influence, widths[1:])
    near_sent = lax.ppermute(near_slab, "tile", near)
    for piece in rest:
        far_slabs.append(lax.ppermute(piece, "tile", far))
    transform, phase, valid = prepare(valid_mask, commands, near_sent, influence, amplitude, aberration)
    parts, far_cmds = [], None
    for k, (first, size) in enumerate(zip(firsts, sizes)):
        earlier = parts[-1:]
        found = spot_slopes(valid, far_cmds, far_slabs[k], transform, phase, first, size, earlier)
        parts.append(found[0])
        if k == 0:
            far_cmds = found[1]
    slopes = parts[-1].reshape(2 * subs, -1)
    groups = [list(range(side, count, 2)) for side in range(2)]
    copies = jnp.broadcast_to(slopes, (count // 2, *slopes.shape))
    same = lax.all_to_all(copies, "tile", 0, 0, axis_index_groups=groups)
    other = lax.ppermute(same, "tile", near)
    return decode(hadamard.T, stroke, same, other)


def solution(mesh):
    placed = (
        P(None, "tile"),
        P(("group", "tile")),
        P(None, ("group", "tile"), None),
        P(("group", "tile"), None, None),
        P(("group", "tile"), None, None),
        P(("group", "tile")),
    )
    return jax.shard_map(
        interaction,
        mesh=mesh,
        in_specs=placed,
        out_specs=P(("group", "tile"), None, None),
        check_vma=False,
    )
```

time: 52.4 us -> 51.9 us (level)
  Pallas kernels: 18.9 us -> 16.4 us
  blocking collectives: 28.3 us -> 29.7 us
  starting transfers between devices: 3.27 us -> 3.94 us
    pallas_call x4 -> x5, Pallas kernels: 10.7 us -> 8.3 us  [spot_slopes(): pl.pallas_call(lambda *refs: spots_kernel(first, lead, len(earlier), *ref...]
    all_to_all x1, blocking collectives: 28.3 us -> 29.7 us  [interaction(): same = lax.all_to_all(copies, 'tile', 0, 0, axis_index_groups=groups)]
    ppermute x3 -> x4, starting transfers between devices: 2.04 us -> 2.7 us  [interaction(): far_slabs.append(lax.ppermute(piece, 'tile', far))]
  transfers between devices with their start and end apart: 6 -> 7, of which waited for: 1 -> 1; matrix products, arithmetic and copies ran while one was open for 0% -> 0% of each run, Pallas kernels for 24% -> 23%
where the time goes in v4:
time: 51.9 us; the launch traced here: 51.6 us
  blocking collectives  29.7 us (57%)
  Pallas kernels  16.4 us (32%)
  starting transfers between devices  3.94 us (8%)
  waiting for transfers between devices  1.36 us (3%)
    all_to_all x1, blocking collectives, interaction(): same = lax.all_to_all(copies, 'tile', 0, 0, axis_index_groups=groups)  29.7 us
    pallas_call x5, Pallas kernels, spot_slopes(): pl.pallas_call(lambda *refs: spots_kernel(first, lead, len(earlier), *ref...  8.3 us
    pallas_call x1, Pallas kernels, prepare(): pl.pallas_call(prepare_kernel, in_specs=[pl.BlockSpec(memory_space=pltpu....  4.52 us
    ppermute x4, starting transfers between devices, interaction(): far_slabs.append(lax.ppermute(piece, 'tile', far))  2.7 us
    pallas_call x1, Pallas kernels, pack_rest(): pl.pallas_call(pack_rest_kernel, in_specs=[whole, pl.BlockSpec(memory_spa...  1.55 us
    ppermute x1, waiting for transfers between devices, interaction(): other = lax.ppermute(same, 'tile', near)  1.35 us
    pallas_call x1, Pallas kernels, pack_first(): pl.pallas_call(pack_first_kernel, in_specs=[far_off] * 3, out_specs=[whol...  1.1 us
  transfers between devices with their start and end apart: 7, of which 1 were waited for; matrix products, arithmetic and copies ran while one was open for 0% of the time, Pallas kernels for 23%

profile of v4, /device:TPU:0, one launch (start us, length us, event | category | flops | bytes accessed | tf_op | source)
XLA Modules:
  0.0 51.6 jit_solution(5990183009710060985)
XLA Ops:
  0.0 1.1 %pack_first.1 = (bf16[72,2176]{1,0:T(8,128)(2,1)S(1)}, bf16[72,128]{1,0:T(8,128)(2,1)S(1)}) custom-call(s32[72,128]{1,0:T(8,128)} %bitcast.9, f32[72]{0:T(128)} %stroke_hbm.1, bf16[3,72,8192]{2,1,0:T(8,128)(2,1)} %influence.5), custom_call_target="tpu_custom_call" | custom-call | tf_op jit(solution)/shard_map/pack_first/pallas_call | solution.py:309
  1.1 1.5 %pack_rest.1 = (bf16[72,2048]{1,0:T(8,128)(2,1)S(1)}, bf16[72,2048]{1,0:T(8,128)(2,1)S(1)}, bf16[72,1024]{1,0:T(8,128)(2,1)S(1)}, bf16[72,1024]{1,0:T(8,128)(2,1)S(1)}, bf16[72,8320]{1,0:T(8,128)(2,1)S(1)}) custom-call(bf16[72,128]{1,0:T(8,128)(2,1)S(1)} %get-tuple-element.17.cmds_ref, bf16[3,72,8192]{2,1,0:T(8,128)(2,1)} %influence.5), custom_call_target="tpu_custom_call" | custom-call | tf_op jit(solution)/shard_map/pack_rest/pallas_call | solution.py:351
  2.7 0.6 %collective-permute-start = (bf16[72,8320]{1,0:T(8,128)(2,1)S(1)}, bf16[72,8320]{1,0:T(8,128)(2,1)S(1)}, u32[]{:S(2)}, u32[]{:S(2)}) collective-permute-start(bf16[72,8320]{1,0:T(8,128)(2,1)S(1)} %get-tuple-element.18), channel_id=1, source_target_pairs={{0,1},{1,0},{2,3},{3,2},{4,5},{5,4},{6,7},{7,6},{8,9},{9,8},{10,11... | collective-permute-start | bytes 3594248 | tf_op jit(solution)/shard_map/ppermute | solution.py:385
  3.2 0.7 %collective-permute-start.1 = (bf16[72,2176]{1,0:T(8,128)(2,1)S(1)}, bf16[72,2176]{1,0:T(8,128)(2,1)S(1)}, u32[]{:S(2)}, u32[]{:S(2)}) collective-permute-start(bf16[72,2176]{1,0:T(8,128)(2,1)S(1)} %get-tuple-element.20), channel_id=1, source_target_pairs={{1,2},{2,1},{3,4},{4,3},{5,6},{6,5},{7,8},{8,7},{9,10},{10,9},{11,... | collective-permute-start | bytes 940040 | tf_op jit(solution)/shard_map/ppermute | solution.py:383
  3.9 0.7 %collective-permute-start.5 = (bf16[72,2048]{1,0:T(8,128)(2,1)S(1)}, bf16[72,2048]{1,0:T(8,128)(2,1)S(1)}, u32[]{:S(2)}, u32[]{:S(2)}) collective-permute-start(bf16[72,2048]{1,0:T(8,128)(2,1)S(1)} %get-tuple-element.27), channel_id=1, source_target_pairs={{1,2},{2,1},{3,4},{4,3},{5,6},{6,5},{7,8},{8,7},{9,10},{10,9},{11,... | collective-permute-start | bytes 884744 | tf_op jit(solution)/shard_map/ppermute | solution.py:387
  4.6 0.7 %collective-permute-start.4 = (bf16[72,2048]{1,0:T(8,128)(2,1)S(1)}, bf16[72,2048]{1,0:T(8,128)(2,1)S(1)}, u32[]{:S(2)}, u32[]{:S(2)}) collective-permute-start(bf16[72,2048]{1,0:T(8,128)(2,1)S(1)} %get-tuple-element.26), channel_id=1, source_target_pairs={{1,2},{2,1},{3,4},{4,3},{5,6},{6,5},{7,8},{8,7},{9,10},{10,9},{11,... | collective-permute-start | bytes 884744 | tf_op jit(solution)/shard_map/ppermute | solution.py:387
  5.3 0.7 %collective-permute-start.2 = (bf16[72,1024]{1,0:T(8,128)(2,1)S(1)}, bf16[72,1024]{1,0:T(8,128)(2,1)S(1)}, u32[]{:S(2)}, u32[]{:S(2)}) collective-permute-start(bf16[72,1024]{1,0:T(8,128)(2,1)S(1)} %get-tuple-element.24), channel_id=1, source_target_pairs={{1,2},{2,1},{3,4},{4,3},{5,6},{6,5},{7,8},{8,7},{9,10},{10,9},{11,... | collective-permute-start | bytes 442376 | tf_op jit(solution)/shard_map/ppermute | solution.py:387
  6.0 0.0 collective-permute-done.near_ref
  6.0 0.7 %collective-permute-start.3 = (bf16[72,1024]{1,0:T(8,128)(2,1)S(1)}, bf16[72,1024]{1,0:T(8,128)(2,1)S(1)}, u32[]{:S(2)}, u32[]{:S(2)}) collective-permute-start(bf16[72,1024]{1,0:T(8,128)(2,1)S(1)} %get-tuple-element.25), channel_id=1, source_target_pairs={{1,2},{2,1},{3,4},{4,3},{5,6},{6,5},{7,8},{8,7},{9,10},{10,9},{11,... | collective-permute-start | bytes 442376 | tf_op jit(solution)/shard_map/ppermute | solution.py:387
  6.7 0.0 copy-done
  6.7 0.0 copy-done.2
  6.7 0.0 copy-done.3
  6.7 0.0 copy-done.5
  6.7 4.5 %prepare.1 = (bf16[32,512,256]{2,1,0:T(8,128)(2,1)S(1)}, f32[32,128,256]{2,1,0:T(8,128)S(1)}, f32[32,128]{1,0:T(8,128)S(1)}) custom-call(s32[32]{0:T(128)S(1)} %copy-done.5, bf16[72,128]{1,0:T(8,128)(2,1)S(1)} %get-tuple-element.17.cmds_ref, bf16[72,8320]{1,0:T(8,128)(2,1)S(1)} %collective-permute-done.near_ref, f32[256,32]{1,0:T(8,128)S(1)} %bitcast.11, ...), custom_call_target="tpu_custom_call" | custom-call | flops 1000000000 | bytes 8388608 | tf_op jit(solution)/shard_map/prepare/pallas_call | solution.py:116
  11.2 0.0 collective-permute-done.1.refs_1_.refs_2_
  11.2 2.1 %spots.5 = (bf16[2,8,128]{2,1,0:T(8,128)(2,1)S(1)}, bf16[128,72]{1,0:T(8,128)(2,1)S(1)}) custom-call(f32[32,128]{1,0:T(8,128)S(1)} %get-tuple-element.19.refs_0_, bf16[72,2176]{1,0:T(8,128)(2,1)S(1)} %collective-permute-done.1.refs_1_.refs_2_, bf16[72,2176]{1,0:T(8,128)(2,1)S(1)} %collective-permute-done.1.refs_1_.refs_2_, ...), custom_call_target="tpu_custom_call" | custom-call | flops 800000000 | bytes 1000000 | tf_op jit(solution)/shard_map/spots/pallas_call | solution.py:228
  13.4 0.0 collective-permute-done.5.refs_2_
  13.4 2.0 %spots.6.refs_5_ = bf16[2,16,128]{2,1,0:T(8,128)(2,1)S(1)} custom-call(f32[32,128]{1,0:T(8,128)S(1)} %get-tuple-element.19.refs_0_, bf16[128,72]{1,0:T(8,128)(2,1)S(1)} %get-tuple-element.23.refs_1_, bf16[72,2048]{1,0:T(8,128)(2,1)S(1)} %collective-permute-done.5.refs_2_, bf16[32,512,256]{2,1,0:T(8,128)(2,1)S(1)} %get-tuple-element.21.refs_3_, ...), custom_call_target="tpu_custom_call" | custom-call | flops 800000000 | bytes 1000000 | tf_op jit(solution)/shard_map/spots/pallas_call | solution.py:228
  15.4 0.0 collective-permute-done.4.refs_2_
  15.4 2.0 %spots.7.refs_5_ = bf16[2,24,128]{2,1,0:T(8,128)(2,1)S(1)} custom-call(f32[32,128]{1,0:T(8,128)S(1)} %get-tuple-element.19.refs_0_, bf16[128,72]{1,0:T(8,128)(2,1)S(1)} %get-tuple-element.23.refs_1_, bf16[72,2048]{1,0:T(8,128)(2,1)S(1)} %collective-permute-done.4.refs_2_, bf16[32,512,256]{2,1,0:T(8,128)(2,1)S(1)} %get-tuple-element.21.refs_3_, ...), custom_call_target="tpu_custom_call" | custom-call | flops 800000000 | bytes 1000000 | tf_op jit(solution)/shard_map/spots/pallas_call | solution.py:228
  17.4 0.0 collective-permute-done.3.refs_2_
  17.4 1.1 %spots.8.refs_5_ = bf16[2,28,128]{2,1,0:T(8,128)(2,1)S(1)} custom-call(f32[32,128]{1,0:T(8,128)S(1)} %get-tuple-element.19.refs_0_, bf16[128,72]{1,0:T(8,128)(2,1)S(1)} %get-tuple-element.23.refs_1_, bf16[72,1024]{1,0:T(8,128)(2,1)S(1)} %collective-permute-done.3.refs_2_, bf16[32,512,256]{2,1,0:T(8,128)(2,1)S(1)} %get-tuple-element.21.refs_3_, ...), custom_call_target="tpu_custom_call" | custom-call | flops 400000000 | bytes 1000000 | tf_op jit(solution)/shard_map/spots/pallas_call | solution.py:228
  18.5 0.0 copy-start.1
  18.5 0.0 copy-start.4
  18.5 0.0 collective-permute-done.2.refs_2_
  18.5 1.1 %spots.9 = bf16[2,32,128]{2,1,0:T(8,128)(2,1)S(1)} custom-call(f32[32,128]{1,0:T(8,128)S(1)} %get-tuple-element.19.refs_0_, bf16[128,72]{1,0:T(8,128)(2,1)S(1)} %get-tuple-element.23.refs_1_, bf16[72,1024]{1,0:T(8,128)(2,1)S(1)} %collective-permute-done.2.refs_2_, bf16[32,512,256]{2,1,0:T(8,128)(2,1)S(1)} %get-tuple-element.21.refs_3_, ...), custom_call_target="tpu_custom_call" | custom-call | flops 400000000 | bytes 1000000 | tf_op jit(solution)/shard_map/spots/pallas_call | solution.py:228
  19.7 29.7 %all_to_all.5.same_ref = bf16[8,64,128]{2,1,0:T(8,128)(2,1)S(1)} all-to-all(bf16[8,64,128]{2,1,0:T(8,128)(2,1)S(1)} %broadcast_in_dim.3), channel_id=1, replica_groups={{0,2,4,6,8,10,12,14},{1,3,5,7,9,11,13,15},{16,18,20,22,24,26,28,30},{17..., dimensions={0} | all-to-all | bytes 262144 | tf_op jit(solution)/shard_map/all_to_all | solution.py:399
  49.3 0.0 collective-permute-start.6
  49.3 1.3 %collective-permute-done.6.other_ref = bf16[8,64,128]{2,1,0:T(8,128)(2,1)S(1)} collective-permute-done((bf16[8,64,128]{2,1,0:T(8,128)(2,1)S(1)}, bf16[8,64,128]{2,1,0:T(8,128)(2,1)S(1)}, u32[]{:S(2)}, u32[]{:S(2)}) %collective-permute-start.6) | collective-permute-done | bytes 131104 | tf_op jit(solution)/shard_map/ppermute | solution.py:400
  50.7 0.0 copy-done.1
  50.7 0.0 copy-done.4
  50.7 1.0 %decode.1 = f32[72,2,512]{2,1,0:T(2,128)} custom-call(s32[72,128]{1,0:T(8,128)S(1)} %bitcast.10, f32[1,72]{1,0:T(1,128)S(1)} %bitcast.14, bf16[8,64,128]{2,1,0:T(8,128)(2,1)S(1)} %all_to_all.5.same_ref, bf16[8,64,128]{2,1,0:T(8,128)(2,1)S(1)} %collective-permute-done.6.other_ref), custom_call_target="tpu_custom_call" | custom-call | tf_op jit(solution)/shard_map/decode/pallas_call | solution.py:267
  (5 shorter events, 0.0 us)
Async XLA Ops:
  0.0 6.7 %copy-start = (f32[512,256]{1,0:T(8,128)S(1)}, f32[512,256]{1,0:T(8,128)}, u32[]{:S(2)}) copy-start(f32[512,256]{1,0:T(8,128)} %constant.2.clone.table_ref) | copy-start | bytes 1572868
  0.0 6.7 %copy-start.2 = (f32[32,16,16]{0,2,1:T(8,128)S(1)}, f32[32,16,16]{0,2,1:T(8,128)}, u32[]{:S(2)}) copy-start(f32[32,16,16]{0,2,1:T(8,128)} %param.10) | copy-start | bytes 98308
  0.0 6.7 %copy-start.3 = (f32[32,16,16]{0,2,1:T(8,128)S(1)}, f32[32,16,16]{0,2,1:T(8,128)}, u32[]{:S(2)}) copy-start(f32[32,16,16]{0,2,1:T(8,128)} %param.11) | copy-start | bytes 98308
  0.0 6.7 %copy-start.5 = (s32[32]{0:T(128)S(1)}, s32[32]{0:T(128)}, u32[]{:S(2)}) copy-start(s32[32]{0:T(128)} %mask_ref.1) | copy-start | bytes 388
  2.7 3.3 %collective-permute-start = (bf16[72,8320]{1,0:T(8,128)(2,1)S(1)}, bf16[72,8320]{1,0:T(8,128)(2,1)S(1)}, u32[]{:S(2)}, u32[]{:S(2)}) collective-permute-start(bf16[72,8320]{1,0:T(8,128)(2,1)S(1)} %get-tuple-element.18), channel_id=1, source_target_pairs={{0,1},{1,0},{2,3},{3,2},{4,5},{5,4},{6,7},{7,6},{8,9},{9,8},{10,11... | collective-permute-start | bytes 3594248 | tf_op jit(solution)/shard_map/ppermute | solution.py:385
  3.2 8.0 %collective-permute-start.1 = (bf16[72,2176]{1,0:T(8,128)(2,1)S(1)}, bf16[72,2176]{1,0:T(8,128)(2,1)S(1)}, u32[]{:S(2)}, u32[]{:S(2)}) collective-permute-start(bf16[72,2176]{1,0:T(8,128)(2,1)S(1)} %get-tuple-element.20), channel_id=1, source_target_pairs={{1,2},{2,1},{3,4},{4,3},{5,6},{6,5},{7,8},{8,7},{9,10},{10,9},{11,... | collective-permute-start | bytes 940040 | tf_op jit(solution)/shard_map/ppermute | solution.py:383
  3.9 9.5 %collective-permute-start.5 = (bf16[72,2048]{1,0:T(8,128)(2,1)S(1)}, bf16[72,2048]{1,0:T(8,128)(2,1)S(1)}, u32[]{:S(2)}, u32[]{:S(2)}) collective-permute-start(bf16[72,2048]{1,0:T(8,128)(2,1)S(1)} %get-tuple-element.27), channel_id=1, source_target_pairs={{1,2},{2,1},{3,4},{4,3},{5,6},{6,5},{7,8},{8,7},{9,10},{10,9},{11,... | collective-permute-start | bytes 884744 | tf_op jit(solution)/shard_map/ppermute | solution.py:387
  4.6 10.8 %collective-permute-start.4 = (bf16[72,2048]{1,0:T(8,128)(2,1)S(1)}, bf16[72,2048]{1,0:T(8,128)(2,1)S(1)}, u32[]{:S(2)}, u32[]{:S(2)}) collective-permute-start(bf16[72,2048]{1,0:T(8,128)(2,1)S(1)} %get-tuple-element.26), channel_id=1, source_target_pairs={{1,2},{2,1},{3,4},{4,3},{5,6},{6,5},{7,8},{8,7},{9,10},{10,9},{11,... | collective-permute-start | bytes 884744 | tf_op jit(solution)/shard_map/ppermute | solution.py:387
  5.3 13.3 %collective-permute-start.2 = (bf16[72,1024]{1,0:T(8,128)(2,1)S(1)}, bf16[72,1024]{1,0:T(8,128)(2,1)S(1)}, u32[]{:S(2)}, u32[]{:S(2)}) collective-permute-start(bf16[72,1024]{1,0:T(8,128)(2,1)S(1)} %get-tuple-element.24), channel_id=1, source_target_pairs={{1,2},{2,1},{3,4},{4,3},{5,6},{6,5},{7,8},{8,7},{9,10},{10,9},{11,... | collective-permute-start | bytes 442376 | tf_op jit(solution)/shard_map/ppermute | solution.py:387
  6.0 11.4 %collective-permute-start.3 = (bf16[72,1024]{1,0:T(8,128)(2,1)S(1)}, bf16[72,1024]{1,0:T(8,128)(2,1)S(1)}, u32[]{:S(2)}, u32[]{:S(2)}) collective-permute-start(bf16[72,1024]{1,0:T(8,128)(2,1)S(1)} %get-tuple-element.25), channel_id=1, source_target_pairs={{1,2},{2,1},{3,4},{4,3},{5,6},{6,5},{7,8},{8,7},{9,10},{10,9},{11,... | collective-permute-start | bytes 442376 | tf_op jit(solution)/shard_map/ppermute | solution.py:387
  18.5 32.2 %copy-start.1 = (s32[128,72]{0,1:T(8,128)S(1)}, s32[128,72]{0,1:T(8,128)}, u32[]{:S(2)}) copy-start(s32[128,72]{0,1:T(8,128)} %param.7) | copy-start | bytes 110596
  18.5 32.1 %copy-start.4 = (f32[72]{0:T(128)S(1)}, f32[72]{0:T(128)}, u32[]{:S(2)}) copy-start(f32[72]{0:T(128)} %stroke_hbm.1) | copy-start | bytes 868
  49.3 1.3 %collective-permute-start.6 = (bf16[8,64,128]{2,1,0:T(8,128)(2,1)S(1)}, bf16[8,64,128]{2,1,0:T(8,128)(2,1)S(1)}, u32[]{:S(2)}, u32[]{:S(2)}) collective-permute-start(bf16[8,64,128]{2,1,0:T(8,128)(2,1)S(1)} %all_to_all.5.same_ref), channel_id=1, source_target_pairs={{0,1},{1,0},{2,3},{3,2},{4,5},{5,4},{6,7},{7,6},{8,9},{9,8},{10,11... | collective-permute-start | bytes 393224 | tf_op jit(solution)/shard_map/ppermute | solution.py:400

commit v5 on v4

--- a/solution.py
+++ b/solution.py
@@ -26,7 +26,7 @@
     root = math.sqrt(2.0)
     return (
         power_fit(root * np.sin(np.pi * r) / r, nodes, 3),
-        power_fit(root * np.cos(np.pi * r), nodes, 3),
+        power_fit(root * np.cos(np.pi * r), nodes, 4),
     )
 
 
@@ -93,7 +93,7 @@
             trans_ref[s, 2 * row + PIX : 2 * row + 2 * PIX] = (lower * real + upper * imag).astype(jnp.bfloat16)
         return carry
 
-    lax.fori_loop(0, subs, fold, 0)
+    lax.fori_loop(0, subs, fold, 0, unroll=4)
     fetch.wait()
 
     def add_terms(g, carry):
@@ -244,21 +244,24 @@
     signs = signs_ref[...].astype(jnp.float32).astype(jnp.bfloat16)
     scale = jnp.broadcast_to(1.0 / (stroke_ref[...] * patterns), (LANES, acts)).T[:, :1]
 
-    def write(even_ref, odd_ref):
+    def write(outer_ref, inner_ref):
         for c in range(2):
             part = slice(c * subs, (c + 1) * subs)
-            slopes = jnp.stack([even_ref[:, part, :], odd_ref[:, part, :]], axis=1)
+            pieces = []
+            for k in range(pairs):
+                ends = [outer_ref[k, part, :], inner_ref[k, part, :]]
+                pieces += ends if k % 2 == 0 else ends[::-1]
             summed = lax.dot_general(
                 signs,
-                slopes.reshape(2 * pairs * subs, patterns),
+                jnp.concatenate(pieces, axis=0),
                 (((1,), (1,)), ((), ())),
                 preferred_element_type=jnp.float32,
             )
             out_ref[:, c, :] = summed * scale
 
-    parity = tile_parity()
-    pl.when(parity == 0)(lambda: write(same_ref, other_ref))
-    pl.when(parity == 1)(lambda: write(other_ref, same_ref))
+    side = tile_side()
+    pl.when(side == 0)(lambda: write(same_ref, other_ref))
+    pl.when(side == 1)(lambda: write(other_ref, same_ref))
 
 
 def decode(signs, stroke, same, other):
@@ -276,6 +279,10 @@
 
 def tile_parity():
     return lax.rem(lax.axis_index("tile"), 2)
+
+
+def tile_side():
+    return lax.rem(lax.div(lax.axis_index("tile") + 1, 2), 2)
 
 
 def in_hbm(value):
@@ -394,7 +401,7 @@
         if k == 0:
             far_cmds = found[1]
     slopes = parts[-1].reshape(2 * subs, -1)
-    groups = [list(range(side, count, 2)) for side in range(2)]
+    groups = [[t for t in range(count) if (t + 1) // 2 % 2 == side] for side in range(2)]
     copies = jnp.broadcast_to(slopes, (count // 2, *slopes.shape))
     same = lax.all_to_all(copies, "tile", 0, 0, axis_index_groups=groups)
     other = lax.ppermute(same, "tile", near)

time: 51.9 us -> 51 us (0.983)
  blocking collectives: 29.7 us -> 25.4 us
  starting transfers between devices: 3.94 us -> 7.54 us
    all_to_all x1, blocking collectives: 29.7 us -> 25.4 us  [interaction(): same = lax.all_to_all(copies, 'tile', 0, 0, axis_index_groups=groups)]
    ppermute x1, starting transfers between devices: 0.01 us -> 3.6 us  [interaction(): other = lax.ppermute(same, 'tile', near)]
where the time goes in v5:
time: 51 us; the launch traced here: 50.7 us
  blocking collectives  25.4 us (50%)
  Pallas kernels  16.5 us (32%)
  starting transfers between devices  7.54 us (15%)
  waiting for transfers between devices  1 us (2%)
    all_to_all x1, blocking collectives, interaction(): same = lax.all_to_all(copies, 'tile', 0, 0, axis_index_groups=groups)  25.4 us
    pallas_call x5, Pallas kernels, spot_slopes(): pl.pallas_call(lambda *refs: spots_kernel(first, lead, len(earlier), *ref...  8.46 us
    pallas_call x1, Pallas kernels, prepare(): pl.pallas_call(prepare_kernel, in_specs=[pl.BlockSpec(memory_space=pltpu....  4.4 us
    ppermute x1, starting transfers between devices, interaction(): other = lax.ppermute(same, 'tile', near)  3.6 us
    ppermute x4, starting transfers between devices, interaction(): far_slabs.append(lax.ppermute(piece, 'tile', far))  2.7 us
    pallas_call x1, Pallas kernels, pack_rest(): pl.pallas_call(pack_rest_kernel, in_specs=[whole, pl.BlockSpec(memory_spa...  1.55 us
    pallas_call x1, Pallas kernels, pack_first(): pl.pallas_call(pack_first_kernel, in_specs=[far_off] * 3, out_specs=[whol...  1.1 us
  transfers between devices with their start and end apart: 7, of which 1 were waited for; matrix products, arithmetic and copies ran while one was open for 0% of the time, Pallas kernels for 23%

profile of v5, /device:TPU:0, one launch (start us, length us, event | category | flops | bytes accessed | tf_op | source)
XLA Modules:
  0.0 50.7 jit_solution(1604275563849702340)
XLA Ops:
  0.0 1.1 %pack_first.1 = (bf16[72,2176]{1,0:T(8,128)(2,1)S(1)}, bf16[72,128]{1,0:T(8,128)(2,1)S(1)}) custom-call(s32[72,128]{1,0:T(8,128)} %bitcast.9, f32[72]{0:T(128)} %stroke_hbm.1, bf16[3,72,8192]{2,1,0:T(8,128)(2,1)} %influence.5), custom_call_target="tpu_custom_call" | custom-call | tf_op jit(solution)/shard_map/pack_first/pallas_call | solution.py:316
  1.1 1.5 %pack_rest.1 = (bf16[72,2048]{1,0:T(8,128)(2,1)S(1)}, bf16[72,2048]{1,0:T(8,128)(2,1)S(1)}, bf16[72,1024]{1,0:T(8,128)(2,1)S(1)}, bf16[72,1024]{1,0:T(8,128)(2,1)S(1)}, bf16[72,8320]{1,0:T(8,128)(2,1)S(1)}) custom-call(bf16[72,128]{1,0:T(8,128)(2,1)S(1)} %get-tuple-element.17.cmds_ref, bf16[3,72,8192]{2,1,0:T(8,128)(2,1)} %influence.5), custom_call_target="tpu_custom_call" | custom-call | tf_op jit(solution)/shard_map/pack_rest/pallas_call | solution.py:358
  2.7 0.6 %collective-permute-start = (bf16[72,8320]{1,0:T(8,128)(2,1)S(1)}, bf16[72,8320]{1,0:T(8,128)(2,1)S(1)}, u32[]{:S(2)}, u32[]{:S(2)}) collective-permute-start(bf16[72,8320]{1,0:T(8,128)(2,1)S(1)} %get-tuple-element.18), channel_id=1, source_target_pairs={{0,1},{1,0},{2,3},{3,2},{4,5},{5,4},{6,7},{7,6},{8,9},{9,8},{10,11... | collective-permute-start | bytes 3594248 | tf_op jit(solution)/shard_map/ppermute | solution.py:392
  3.2 0.7 %collective-permute-start.1 = (bf16[72,2176]{1,0:T(8,128)(2,1)S(1)}, bf16[72,2176]{1,0:T(8,128)(2,1)S(1)}, u32[]{:S(2)}, u32[]{:S(2)}) collective-permute-start(bf16[72,2176]{1,0:T(8,128)(2,1)S(1)} %get-tuple-element.20), channel_id=1, source_target_pairs={{1,2},{2,1},{3,4},{4,3},{5,6},{6,5},{7,8},{8,7},{9,10},{10,9},{11,... | collective-permute-start | bytes 940040 | tf_op jit(solution)/shard_map/ppermute | solution.py:390
  3.9 0.7 %collective-permute-start.5 = (bf16[72,2048]{1,0:T(8,128)(2,1)S(1)}, bf16[72,2048]{1,0:T(8,128)(2,1)S(1)}, u32[]{:S(2)}, u32[]{:S(2)}) collective-permute-start(bf16[72,2048]{1,0:T(8,128)(2,1)S(1)} %get-tuple-element.27), channel_id=1, source_target_pairs={{1,2},{2,1},{3,4},{4,3},{5,6},{6,5},{7,8},{8,7},{9,10},{10,9},{11,... | collective-permute-start | bytes 884744 | tf_op jit(solution)/shard_map/ppermute | solution.py:394
  4.6 0.7 %collective-permute-start.4 = (bf16[72,2048]{1,0:T(8,128)(2,1)S(1)}, bf16[72,2048]{1,0:T(8,128)(2,1)S(1)}, u32[]{:S(2)}, u32[]{:S(2)}) collective-permute-start(bf16[72,2048]{1,0:T(8,128)(2,1)S(1)} %get-tuple-element.26), channel_id=1, source_target_pairs={{1,2},{2,1},{3,4},{4,3},{5,6},{6,5},{7,8},{8,7},{9,10},{10,9},{11,... | collective-permute-start | bytes 884744 | tf_op jit(solution)/shard_map/ppermute | solution.py:394
  5.3 0.7 %collective-permute-start.2 = (bf16[72,1024]{1,0:T(8,128)(2,1)S(1)}, bf16[72,1024]{1,0:T(8,128)(2,1)S(1)}, u32[]{:S(2)}, u32[]{:S(2)}) collective-permute-start(bf16[72,1024]{1,0:T(8,128)(2,1)S(1)} %get-tuple-element.24), channel_id=1, source_target_pairs={{1,2},{2,1},{3,4},{4,3},{5,6},{6,5},{7,8},{8,7},{9,10},{10,9},{11,... | collective-permute-start | bytes 442376 | tf_op jit(solution)/shard_map/ppermute | solution.py:394
  6.0 0.0 collective-permute-done.near_ref
  6.0 0.7 %collective-permute-start.3 = (bf16[72,1024]{1,0:T(8,128)(2,1)S(1)}, bf16[72,1024]{1,0:T(8,128)(2,1)S(1)}, u32[]{:S(2)}, u32[]{:S(2)}) collective-permute-start(bf16[72,1024]{1,0:T(8,128)(2,1)S(1)} %get-tuple-element.25), channel_id=1, source_target_pairs={{1,2},{2,1},{3,4},{4,3},{5,6},{6,5},{7,8},{8,7},{9,10},{10,9},{11,... | collective-permute-start | bytes 442376 | tf_op jit(solution)/shard_map/ppermute | solution.py:394
  6.7 0.0 copy-done
  6.7 0.0 copy-done.2
  6.7 0.0 copy-done.3
  6.7 0.0 copy-done.5
  6.7 4.4 %prepare.1 = (bf16[32,512,256]{2,1,0:T(8,128)(2,1)S(1)}, f32[32,128,256]{2,1,0:T(8,128)S(1)}, f32[32,128]{1,0:T(8,128)S(1)}) custom-call(s32[32]{0:T(128)S(1)} %copy-done.5, bf16[72,128]{1,0:T(8,128)(2,1)S(1)} %get-tuple-element.17.cmds_ref, bf16[72,8320]{1,0:T(8,128)(2,1)S(1)} %collective-permute-done.near_ref, f32[256,32]{1,0:T(8,128)S(1)} %bitcast.11, ...), custom_call_target="tpu_custom_call" | custom-call | flops 1000000000 | bytes 8388608 | tf_op jit(solution)/shard_map/prepare/pallas_call | solution.py:116
  11.1 0.0 collective-permute-done.1.refs_1_.refs_2_
  11.1 2.2 %spots.5 = (bf16[2,8,128]{2,1,0:T(8,128)(2,1)S(1)}, bf16[128,72]{1,0:T(8,128)(2,1)S(1)}) custom-call(f32[32,128]{1,0:T(8,128)S(1)} %get-tuple-element.19.refs_0_, bf16[72,2176]{1,0:T(8,128)(2,1)S(1)} %collective-permute-done.1.refs_1_.refs_2_, bf16[72,2176]{1,0:T(8,128)(2,1)S(1)} %collective-permute-done.1.refs_1_.refs_2_, ...), custom_call_target="tpu_custom_call" | custom-call | flops 800000000 | bytes 1000000 | tf_op jit(solution)/shard_map/spots/pallas_call | solution.py:228
  13.3 0.0 collective-permute-done.5.refs_2_
  13.3 2.1 %spots.6.refs_5_ = bf16[2,16,128]{2,1,0:T(8,128)(2,1)S(1)} custom-call(f32[32,128]{1,0:T(8,128)S(1)} %get-tuple-element.19.refs_0_, bf16[128,72]{1,0:T(8,128)(2,1)S(1)} %get-tuple-element.23.refs_1_, bf16[72,2048]{1,0:T(8,128)(2,1)S(1)} %collective-permute-done.5.refs_2_, bf16[32,512,256]{2,1,0:T(8,128)(2,1)S(1)} %get-tuple-element.21.refs_3_, ...), custom_call_target="tpu_custom_call" | custom-call | flops 800000000 | bytes 1000000 | tf_op jit(solution)/shard_map/spots/pallas_call | solution.py:228
  15.4 0.0 collective-permute-done.4.refs_2_
  15.4 2.0 %spots.7.refs_5_ = bf16[2,24,128]{2,1,0:T(8,128)(2,1)S(1)} custom-call(f32[32,128]{1,0:T(8,128)S(1)} %get-tuple-element.19.refs_0_, bf16[128,72]{1,0:T(8,128)(2,1)S(1)} %get-tuple-element.23.refs_1_, bf16[72,2048]{1,0:T(8,128)(2,1)S(1)} %collective-permute-done.4.refs_2_, bf16[32,512,256]{2,1,0:T(8,128)(2,1)S(1)} %get-tuple-element.21.refs_3_, ...), custom_call_target="tpu_custom_call" | custom-call | flops 800000000 | bytes 1000000 | tf_op jit(solution)/shard_map/spots/pallas_call | solution.py:228
  17.4 0.0 collective-permute-done.3.refs_2_
  17.4 1.1 %spots.8.refs_5_ = bf16[2,28,128]{2,1,0:T(8,128)(2,1)S(1)} custom-call(f32[32,128]{1,0:T(8,128)S(1)} %get-tuple-element.19.refs_0_, bf16[128,72]{1,0:T(8,128)(2,1)S(1)} %get-tuple-element.23.refs_1_, bf16[72,1024]{1,0:T(8,128)(2,1)S(1)} %collective-permute-done.3.refs_2_, bf16[32,512,256]{2,1,0:T(8,128)(2,1)S(1)} %get-tuple-element.21.refs_3_, ...), custom_call_target="tpu_custom_call" | custom-call | flops 400000000 | bytes 1000000 | tf_op jit(solution)/shard_map/spots/pallas_call | solution.py:228
  18.5 0.0 copy-start.1
  18.6 0.0 copy-start.4
  18.6 0.0 collective-permute-done.2.refs_2_
  18.6 1.1 %spots.9 = bf16[2,32,128]{2,1,0:T(8,128)(2,1)S(1)} custom-call(f32[32,128]{1,0:T(8,128)S(1)} %get-tuple-element.19.refs_0_, bf16[128,72]{1,0:T(8,128)(2,1)S(1)} %get-tuple-element.23.refs_1_, bf16[72,1024]{1,0:T(8,128)(2,1)S(1)} %collective-permute-done.2.refs_2_, bf16[32,512,256]{2,1,0:T(8,128)(2,1)S(1)} %get-tuple-element.21.refs_3_, ...), custom_call_target="tpu_custom_call" | custom-call | flops 400000000 | bytes 1000000 | tf_op jit(solution)/shard_map/spots/pallas_call | solution.py:228
  19.7 25.4 %all_to_all.5.same_ref = bf16[8,64,128]{2,1,0:T(8,128)(2,1)S(1)} all-to-all(bf16[8,64,128]{2,1,0:T(8,128)(2,1)S(1)} %broadcast_in_dim.3), channel_id=1, replica_groups={{0,3,4,7,8,11,12,15},{1,2,5,6,9,10,13,14},{16,19,20,23,24,27,28,31},{17..., dimensions={0} | all-to-all | bytes 262144 | tf_op jit(solution)/shard_map/all_to_all | solution.py:406
  45.1 3.6 %collective-permute-start.6 = (bf16[8,64,128]{2,1,0:T(8,128)(2,1)S(1)}, bf16[8,64,128]{2,1,0:T(8,128)(2,1)S(1)}, u32[]{:S(2)}, u32[]{:S(2)}) collective-permute-start(bf16[8,64,128]{2,1,0:T(8,128)(2,1)S(1)} %all_to_all.5.same_ref), channel_id=1, source_target_pairs={{0,1},{1,0},{2,3},{3,2},{4,5},{5,4},{6,7},{7,6},{8,9},{9,8},{10,11... | collective-permute-start | bytes 393224 | tf_op jit(solution)/shard_map/ppermute | solution.py:407
  48.7 1.0 %collective-permute-done.6.other_ref = bf16[8,64,128]{2,1,0:T(8,128)(2,1)S(1)} collective-permute-done((bf16[8,64,128]{2,1,0:T(8,128)(2,1)S(1)}, bf16[8,64,128]{2,1,0:T(8,128)(2,1)S(1)}, u32[]{:S(2)}, u32[]{:S(2)}) %collective-permute-start.6) | collective-permute-done | bytes 131104 | tf_op jit(solution)/shard_map/ppermute | solution.py:407
  49.7 0.0 copy-done.1
  49.7 0.0 copy-done.4
  49.7 1.0 %decode.1 = f32[72,2,512]{2,1,0:T(2,128)} custom-call(s32[72,128]{1,0:T(8,128)S(1)} %bitcast.10, f32[1,72]{1,0:T(1,128)S(1)} %bitcast.14, bf16[8,64,128]{2,1,0:T(8,128)(2,1)S(1)} %all_to_all.5.same_ref, bf16[8,64,128]{2,1,0:T(8,128)(2,1)S(1)} %collective-permute-done.6.other_ref), custom_call_target="tpu_custom_call" | custom-call | tf_op jit(solution)/shard_map/decode/pallas_call | solution.py:270
  (5 shorter events, 0.0 us)
Async XLA Ops:
  0.0 6.7 %copy-start = (f32[512,256]{1,0:T(8,128)S(1)}, f32[512,256]{1,0:T(8,128)}, u32[]{:S(2)}) copy-start(f32[512,256]{1,0:T(8,128)} %constant.2.clone.table_ref) | copy-start | bytes 1572868
  0.0 6.7 %copy-start.2 = (f32[32,16,16]{0,2,1:T(8,128)S(1)}, f32[32,16,16]{0,2,1:T(8,128)}, u32[]{:S(2)}) copy-start(f32[32,16,16]{0,2,1:T(8,128)} %param.10) | copy-start | bytes 98308
  0.0 6.7 %copy-start.3 = (f32[32,16,16]{0,2,1:T(8,128)S(1)}, f32[32,16,16]{0,2,1:T(8,128)}, u32[]{:S(2)}) copy-start(f32[32,16,16]{0,2,1:T(8,128)} %param.11) | copy-start | bytes 98308
  0.0 6.7 %copy-start.5 = (s32[32]{0:T(128)S(1)}, s32[32]{0:T(128)}, u32[]{:S(2)}) copy-start(s32[32]{0:T(128)} %mask_ref.1) | copy-start | bytes 388
  2.7 3.3 %collective-permute-start = (bf16[72,8320]{1,0:T(8,128)(2,1)S(1)}, bf16[72,8320]{1,0:T(8,128)(2,1)S(1)}, u32[]{:S(2)}, u32[]{:S(2)}) collective-permute-start(bf16[72,8320]{1,0:T(8,128)(2,1)S(1)} %get-tuple-element.18), channel_id=1, source_target_pairs={{0,1},{1,0},{2,3},{3,2},{4,5},{5,4},{6,7},{7,6},{8,9},{9,8},{10,11... | collective-permute-start | bytes 3594248 | tf_op jit(solution)/shard_map/ppermute | solution.py:392
  3.2 7.9 %collective-permute-start.1 = (bf16[72,2176]{1,0:T(8,128)(2,1)S(1)}, bf16[72,2176]{1,0:T(8,128)(2,1)S(1)}, u32[]{:S(2)}, u32[]{:S(2)}) collective-permute-start(bf16[72,2176]{1,0:T(8,128)(2,1)S(1)} %get-tuple-element.20), channel_id=1, source_target_pairs={{1,2},{2,1},{3,4},{4,3},{5,6},{6,5},{7,8},{8,7},{9,10},{10,9},{11,... | collective-permute-start | bytes 940040 | tf_op jit(solution)/shard_map/ppermute | solution.py:390
  3.9 9.4 %collective-permute-start.5 = (bf16[72,2048]{1,0:T(8,128)(2,1)S(1)}, bf16[72,2048]{1,0:T(8,128)(2,1)S(1)}, u32[]{:S(2)}, u32[]{:S(2)}) collective-permute-start(bf16[72,2048]{1,0:T(8,128)(2,1)S(1)} %get-tuple-element.27), channel_id=1, source_target_pairs={{1,2},{2,1},{3,4},{4,3},{5,6},{6,5},{7,8},{8,7},{9,10},{10,9},{11,... | collective-permute-start | bytes 884744 | tf_op jit(solution)/shard_map/ppermute | solution.py:394
  4.6 10.8 %collective-permute-start.4 = (bf16[72,2048]{1,0:T(8,128)(2,1)S(1)}, bf16[72,2048]{1,0:T(8,128)(2,1)S(1)}, u32[]{:S(2)}, u32[]{:S(2)}) collective-permute-start(bf16[72,2048]{1,0:T(8,128)(2,1)S(1)} %get-tuple-element.26), channel_id=1, source_target_pairs={{1,2},{2,1},{3,4},{4,3},{5,6},{6,5},{7,8},{8,7},{9,10},{10,9},{11,... | collective-permute-start | bytes 884744 | tf_op jit(solution)/shard_map/ppermute | solution.py:394
  5.3 13.3 %collective-permute-start.2 = (bf16[72,1024]{1,0:T(8,128)(2,1)S(1)}, bf16[72,1024]{1,0:T(8,128)(2,1)S(1)}, u32[]{:S(2)}, u32[]{:S(2)}) collective-permute-start(bf16[72,1024]{1,0:T(8,128)(2,1)S(1)} %get-tuple-element.24), channel_id=1, source_target_pairs={{1,2},{2,1},{3,4},{4,3},{5,6},{6,5},{7,8},{8,7},{9,10},{10,9},{11,... | collective-permute-start | bytes 442376 | tf_op jit(solution)/shard_map/ppermute | solution.py:394
  6.0 11.5 %collective-permute-start.3 = (bf16[72,1024]{1,0:T(8,128)(2,1)S(1)}, bf16[72,1024]{1,0:T(8,128)(2,1)S(1)}, u32[]{:S(2)}, u32[]{:S(2)}) collective-permute-start(bf16[72,1024]{1,0:T(8,128)(2,1)S(1)} %get-tuple-element.25), channel_id=1, source_target_pairs={{1,2},{2,1},{3,4},{4,3},{5,6},{6,5},{7,8},{8,7},{9,10},{10,9},{11,... | collective-permute-start | bytes 442376 | tf_op jit(solution)/shard_map/ppermute | solution.py:394
  18.5 31.1 %copy-start.1 = (s32[128,72]{0,1:T(8,128)S(1)}, s32[128,72]{0,1:T(8,128)}, u32[]{:S(2)}) copy-start(s32[128,72]{0,1:T(8,128)} %param.7) | copy-start | bytes 110596
  18.6 31.1 %copy-start.4 = (f32[72]{0:T(128)S(1)}, f32[72]{0:T(128)}, u32[]{:S(2)}) copy-start(f32[72]{0:T(128)} %stroke_hbm.1) | copy-start | bytes 868
  45.1 4.6 %collective-permute-start.6 = (bf16[8,64,128]{2,1,0:T(8,128)(2,1)S(1)}, bf16[8,64,128]{2,1,0:T(8,128)(2,1)S(1)}, u32[]{:S(2)}, u32[]{:S(2)}) collective-permute-start(bf16[8,64,128]{2,1,0:T(8,128)(2,1)S(1)} %all_to_all.5.same_ref), channel_id=1, source_target_pairs={{0,1},{1,0},{2,3},{3,2},{4,5},{5,4},{6,7},{7,6},{8,9},{9,8},{10,11... | collective-permute-start | bytes 393224 | tf_op jit(solution)/shard_map/ppermute | solution.py:407
